TPU v7x, 128 devices: a whole 4x4x4 slice. The times are simulated.
128 devices in a mesh: rows: 4 (over z), cols: 32 (over x, y, core).
Axes of the slice: x: 4, y: 4, z: 4, core: 2. Of those that a mesh axis runs over, the one named last changes fastest.
Arguments:
- fields: float32 [5, 64, 1024, 512], P(None, None, 'cols', 'rows'), may hold values from -6 to 6
- cotangent: float32 [5, 64, 1024, 512], P(None, None, 'cols', 'rows'), may hold values from -6 to 6
- ocean_mask: int32 [1024, 512], P('cols', 'rows'), may hold values from 0 to 1
- depth_levels: int32 [1024, 512], P('cols', 'rows'), may hold values from 16 to 64
- in_weight: bfloat16 [256, 256], replicated, may hold values from -0.375 to 0.375
- in_bias: float32 [256], replicated, may hold values from -3 to 3
- out_weight: bfloat16 [256, 63], replicated, may hold values from -0.375 to 0.375
Outputs:
- new_fields: float32 [5, 64, 1024, 512], P(None, None, 'cols', 'rows')
- pressure: float32 [64, 1024, 512], P(None, 'cols', 'rows')
- grad_in_weight: float32 [256, 256], replicated
- grad_in_bias: float32 [256], replicated
- grad_out_weight: float32 [256, 63], replicated
All inputs are finite; a program needn't handle non-finite values.
Results may differ from a plain program's by a relative error of at most 0.0059.
Values sent between devices are 32-bit elements; how exact they have to be, the bound alone decides.
A program may use at most 192 MiB of HBM per device.

v0:
```python
import math

import jax
import jax.numpy as jnp
from jax import lax
from jax.sharding import PartitionSpec as P

NZ = 64


TIME_STEP = 0.2
RATE_MAX = 2.0
THERMAL = 0.5
HALINE = 0.5
SPECTRAL_SHIFT = 0.001
WENO_EPS = 1e-06


def padded_2(block, sides, width):
    for axis, dim in sides:
        count = lax.axis_size(axis)
        forward = [(i, i + 1) for i in range(count - 1)]
        backward = [(target, source) for source, target in forward]
        low = lax.ppermute(
            lax.slice_in_dim(block, block.shape[dim] - width, None, axis=dim), axis, forward
        )
        high = lax.ppermute(lax.slice_in_dim(block, 0, width, axis=dim), axis, backward)
        block = jnp.concatenate([low, block, high], axis=dim)
    return block


def weno_face(first, second, third, fourth, fifth):
    cand_low = (2.0 * first - 7.0 * second + 11.0 * third) / 6.0
    cand_mid = (-second + 5.0 * third + 2.0 * fourth) / 6.0
    cand_high = (2.0 * third + 5.0 * fourth - fifth) / 6.0
    rough_low = 13.0 / 12.0 * jnp.square(first - 2.0 * second + third) + 0.25 * jnp.square(
        first - 4.0 * second + 3.0 * third
    )
    rough_mid = 13.0 / 12.0 * jnp.square(second - 2.0 * third + fourth) + 0.25 * jnp.square(
        second - fourth
    )
    rough_high = 13.0 / 12.0 * jnp.square(third - 2.0 * fourth + fifth) + 0.25 * jnp.square(
        3.0 * third - 4.0 * fourth + fifth
    )
    weight_low = 0.1 / jnp.square(WENO_EPS + rough_low)
    weight_mid = 0.6 / jnp.square(WENO_EPS + rough_mid)
    weight_high = 0.3 / jnp.square(WENO_EPS + rough_high)
    return (weight_low * cand_low + weight_mid * cand_mid + weight_high * cand_high) / (
        weight_low + weight_mid + weight_high
    )


def take_cells(array, start, length, along):
    return lax.slice_in_dim(array, start, start + length, axis=along)


def flux_tendency(tracer, velocity, wet_cells, along, length):
    shifted = [take_cells(tracer, offset, length + 1, along) for offset in range(6)]
    left_value = weno_face(shifted[0], shifted[1], shifted[2], shifted[3], shifted[4])
    right_value = weno_face(shifted[5], shifted[4], shifted[3], shifted[2], shifted[1])
    face_speed = 0.5 * (
        take_cells(velocity, 2, length + 1, along) + take_cells(velocity, 3, length + 1, along)
    )
    face_speed = (
        face_speed
        * take_cells(wet_cells, 2, length + 1, along)
        * take_cells(wet_cells, 3, length + 1, along)
    )
    face_flux = (
        jnp.maximum(face_speed, 0.0) * left_value + jnp.minimum(face_speed, 0.0) * right_value
    )
    return take_cells(face_flux, 0, length, along) - take_cells(face_flux, 1, length, along)


def advect_one(tracer, east_speed, north_speed, wet_cells, north_count, east_count):
    inner_rows = slice(3, 3 + north_count)
    inner_cols = slice(3, 3 + east_count)
    along_east = flux_tendency(
        tracer[:, inner_rows, :],
        east_speed[:, inner_rows, :],
        wet_cells[:, inner_rows, :],
        2,
        east_count,
    )
    along_north = flux_tendency(
        tracer[:, :, inner_cols],
        north_speed[:, :, inner_cols],
        wet_cells[:, :, inner_cols],
        1,
        north_count,
    )
    inner = tracer[:, inner_rows, inner_cols]
    return wet_cells[:, inner_rows, inner_cols] * (inner + TIME_STEP * (along_east + along_north))


def advance(extended, north_count, east_count):
    advected = lax.map(
        lambda tracer: advect_one(
            tracer, extended[0], extended[1], extended[5], north_count, east_count
        ),
        extended[:5],
    )
    east_speed = extended[0]
    north_speed = extended[1]
    east_change = (
        east_speed[:, 3 : 3 + north_count, 4 : 4 + east_count]
        - east_speed[:, 3 : 3 + north_count, 2 : 2 + east_count]
    )
    north_change = (
        north_speed[:, 4 : 4 + north_count, 3 : 3 + east_count]
        - north_speed[:, 2 : 2 + north_count, 3 : 3 + east_count]
    )
    return (advected, 0.5 * (east_change + north_change))


def wet_mask(ocean_mask, depth_levels):
    level_ids = jnp.arange(NZ, dtype=jnp.int32)[:, None, None]
    wet_cells = (ocean_mask[None] == 1) & (level_ids < depth_levels[None])
    return wet_cells.astype(jnp.float32)


def vertical_diff(array):
    zero_layer = jnp.zeros_like(array[:1])
    upper = jnp.concatenate([array[1:], zero_layer], 0)
    lower = jnp.concatenate([zero_layer, array[:-1]], 0)
    return 0.5 * (upper - lower)


def mix_column(tracer, rates, wet_cells, bond):
    face_flux = rates * bond * (tracer[1:] - tracer[:-1])
    zero_layer = jnp.zeros_like(face_flux[:1])
    padded = jnp.concatenate([zero_layer, face_flux, zero_layer], 0)
    return wet_cells * (tracer + TIME_STEP * (padded[1:] - padded[:-1]))


def rate_gradient(tracer, grad_tracer, wet_cells, bond):
    weighted = wet_cells * grad_tracer
    return TIME_STEP * (weighted[:-1] - weighted[1:]) * bond * (tracer[1:] - tracer[:-1])


def closure_forward(advected, in_weight, in_bias, out_weight):
    levels = advected.shape[1]
    features = (
        jnp.concatenate([advected[0], advected[1], advected[3], advected[4]], 0)
        .reshape(4 * levels, -1)
        .astype(jnp.bfloat16)
    )
    hidden_pre = (
        lax.dot_general(
            in_weight, features, (((0,), (0,)), ((), ())), preferred_element_type=jnp.float32
        )
        + in_bias[:, None]
    )
    activity = jnp.tanh(hidden_pre)
    hidden = activity.astype(jnp.bfloat16)
    output = lax.dot_general(
        out_weight, hidden, (((0,), (0,)), ((), ())), preferred_element_type=jnp.float32
    )
    rates = RATE_MAX * jax.nn.sigmoid(output)
    return (features, activity, hidden, rates)


def closure_backward(features, activity, hidden, rates, grad_rates, out_weight):
    grad_output = (grad_rates * rates * (1.0 - rates / RATE_MAX)).astype(jnp.bfloat16)
    grad_w_out = lax.dot_general(
        hidden, grad_output, (((1,), (1,)), ((), ())), preferred_element_type=jnp.float32
    )
    grad_pre = jnp.dot(out_weight, grad_output, preferred_element_type=jnp.float32) * (
        1.0 - activity * activity
    )
    grad_b_in = jnp.sum(grad_pre, axis=1)
    grad_w_in = lax.dot_general(
        features,
        grad_pre.astype(jnp.bfloat16),
        (((1,), (1,)), ((), ())),
        preferred_element_type=jnp.float32,
    )
    return (grad_w_in, grad_b_in, grad_w_out)


def column_step(advected, masked, wet_cells, spread, cotangent, in_weight, in_bias, out_weight):
    features, activity, hidden, rates_flat = closure_forward(
        advected, in_weight, in_bias, out_weight
    )
    rates = rates_flat.reshape(wet_cells.shape[0] - 1, wet_cells.shape[1], wet_cells.shape[2])
    bond = wet_cells[:-1] * wet_cells[1:]
    heat = mix_column(advected[3], rates, wet_cells, bond)
    salt = mix_column(advected[4], rates, wet_cells, bond)
    density = THERMAL * heat - HALINE * salt
    forcing = wet_cells * (vertical_diff(density) - (spread + vertical_diff(masked[2])) / TIME_STEP)
    adjoint_source = TIME_STEP * vertical_diff(wet_cells * cotangent[2])
    saved = (features, activity, hidden, rates_flat, bond, heat, salt)
    return (saved, forcing, adjoint_source)


def finish_step(advected, wet_cells, pressure, back, cotangent, saved, out_weight):
    features, activity, hidden, rates_flat, bond, heat, salt = saved
    new_w = wet_cells * (advected[2] - TIME_STEP * vertical_diff(pressure))
    new_fields = jnp.stack([advected[0], advected[1], new_w, heat, salt])
    grad_density = -vertical_diff(wet_cells * back)
    grad_heat = cotangent[3] + THERMAL * grad_density
    grad_salt = cotangent[4] - HALINE * grad_density
    grad_rates = rate_gradient(advected[3], grad_heat, wet_cells, bond) + rate_gradient(
        advected[4], grad_salt, wet_cells, bond
    )
    grads = closure_backward(
        features, activity, hidden, rates_flat, grad_rates.reshape(rates_flat.shape), out_weight
    )
    return (new_fields, grads)


def dct_matrix(length):
    freq = jnp.arange(length, dtype=jnp.float32)[:, None]
    cells = jnp.arange(length, dtype=jnp.float32)[None, :]
    scale = jnp.where(freq == 0.0, jnp.sqrt(1.0 / length), jnp.sqrt(2.0 / length))
    return scale * jnp.cos(math.pi * (cells + 0.5) * freq / length)


def eigen_values(freq, length):
    return 2.0 - 2.0 * jnp.cos(math.pi * freq.astype(jnp.float32) / length)


def spectral_denominator(plane_ids, north_ids, east_ids, north_total, east_total):
    level_part = eigen_values(plane_ids % NZ, NZ)[:, None, None]
    north_part = eigen_values(north_ids, north_total)[None, :, None]
    east_part = eigen_values(east_ids, east_total)[None, None, :]
    return SPECTRAL_SHIFT + level_part + north_part + east_part


def column_swap(block):
    return lax.all_to_all(block, "cols", split_axis=0, concat_axis=1, tiled=True)


def row_swap(block):
    return lax.all_to_all(block, "rows", split_axis=1, concat_axis=2, tiled=True)


def horizontal_pencil(planes):
    high = lax.Precision.HIGHEST
    rows_total = lax.axis_size("rows")
    columns_total = lax.axis_size("cols")
    tile_east = planes.shape[2]
    groups = planes.shape[0] // columns_total
    gathered = column_swap(planes)
    north_total = gathered.shape[1]
    north_matrix = dct_matrix(north_total)
    gathered = jnp.einsum("ky,pyx->pkx", north_matrix, gathered, precision=high)
    lines = row_swap(gathered)
    part_rows = lines.shape[1]
    east_total = lines.shape[2]
    east_matrix = dct_matrix(east_total)
    spectrum = jnp.einsum("pyx,kx->pyk", lines, east_matrix, precision=high)
    plane_ids = lax.axis_index("cols") * groups + jnp.arange(groups, dtype=jnp.int32)
    north_ids = lax.axis_index("rows") * part_rows + jnp.arange(part_rows, dtype=jnp.int32)
    east_ids = jnp.arange(east_total, dtype=jnp.int32)
    spectrum = spectrum / spectral_denominator(
        plane_ids, north_ids, east_ids, north_total, east_total
    )
    back_east = jnp.einsum("pyk,kx->pyx", spectrum, east_matrix, precision=high)
    ordered = (
        back_east.reshape(groups, part_rows, rows_total, tile_east)
        .transpose(0, 2, 1, 3)
        .reshape(groups, north_total, tile_east)
    )
    returned = row_swap(ordered)
    returned = (
        returned.reshape(groups, part_rows, rows_total, tile_east)
        .transpose(0, 2, 1, 3)
        .reshape(groups, north_total, tile_east)
    )
    back_north = jnp.einsum("ky,pkx->pyx", north_matrix, returned, precision=high)
    tile_north = north_total // columns_total
    ordered = (
        back_north.reshape(groups, columns_total, tile_north, tile_east)
        .transpose(1, 0, 2, 3)
        .reshape(columns_total * groups, tile_north, tile_east)
    )
    returned = column_swap(ordered)
    return (
        returned.reshape(groups, columns_total, tile_north, tile_east)
        .transpose(1, 0, 2, 3)
        .reshape(planes.shape)
    )


def spectral_solve(sources):
    high = lax.Precision.HIGHEST
    level_matrix = dct_matrix(NZ)
    levels_done = jnp.einsum("mz,szyx->smyx", level_matrix, sources, precision=high)
    planes = levels_done.reshape(2 * NZ, sources.shape[2], sources.shape[3])
    solved = horizontal_pencil(planes)
    solved = solved.reshape(sources.shape)
    return jnp.einsum("mz,smyx->szyx", level_matrix, solved, precision=high)


def per_device(fields, cotangent, ocean_mask, depth_levels, in_weight, in_bias, out_weight):
    north_count = fields.shape[2]
    east_count = fields.shape[3]
    wet_cells = wet_mask(ocean_mask, depth_levels)
    masked = fields * wet_cells[None]
    stacked = jnp.concatenate([masked, wet_cells[None]], 0)
    extended = padded_2(stacked, (("rows", 3), ("cols", 2)), 3)
    advected, spread = advance(extended, north_count, east_count)
    saved, forcing, adjoint_source = column_step(
        advected, masked, wet_cells, spread, cotangent, in_weight, in_bias, out_weight
    )
    solved = spectral_solve(jnp.stack([forcing, adjoint_source]))
    pressure = solved[0]
    back = solved[1]
    new_fields, grads = finish_step(
        advected, wet_cells, pressure, back, cotangent, saved, out_weight
    )
    grad_w_in, grad_b_in, grad_w_out = lax.psum((grads[0], grads[1], grads[2]), ("rows", "cols"))
    return (new_fields, pressure, grad_w_in, grad_b_in, grad_w_out)


def solution(mesh):
    in_specs = (
        P(None, None, "cols", "rows"),
        P(None, None, "cols", "rows"),
        P("cols", "rows"),
        P("cols", "rows"),
        P(),
        P(),
        P(),
    )
    out_specs = (P(None, None, "cols", "rows"), P(None, "cols", "rows"), P(), P(), P())
    return jax.shard_map(
        per_device, mesh=mesh, in_specs=in_specs, out_specs=out_specs, check_vma=False
    )
```

profile of v0, /device:TPU:0, one launch (start us, length us, event | category | flops | bytes accessed | tf_op | source)
XLA Modules:
  0.0 809.7 jit_solution(18267483434153150861)
XLA Ops:
  9.8 5.6 copy_multiply_fusion
  15.4 6.0 slice_maximum_fusion
  40.4 4.7 collective-permute-done.1
  61.3 9.5 %pad_maximum_fusion = f32[6,64,38,134]{3,1,2,0:T(8,128)S(1)} fusion(f32[6,64,3,134]{3,1,2,0:T(8,128)S(1)} %collective-permute-done.3, f32[6,64,32,3]{3,1,2,0:T(8,128)} %copy.109, f32[1,64,32,128]{3,1,2,0:T(8,128)S(1)} %fusion.130, f32[5,64,32,128]{3,1,2,0:T(8,128)S(1)} %bitcast.179, f32[6,64,32,3]{3,1,2,0:T(8,128)S(1)} %copy-done.6, ...), kind=kLoop, calls=%fused_computation.71 | loop fusion | flops 9776640 | bytes 15642624 | tf_op jit(solution)/shard_map/concatenate | solution.py:28
  70.8 5.3 copy-done.1
  77.9 20.1 %copy.110 = f32[6,64,38,134]{3,2,1,0:T(8,128)} copy(f32[6,64,38,134]{3,1,2,0:T(8,128)} %copy-done.1) | data formatting | bytes 15642624 | tf_op jit(solution)/shard_map/while | solution.py:97
  97.9 11.3 %slice.389 = f32[5,64,38,134]{3,1,2,0:T(8,128)} slice(f32[6,64,38,134]{3,1,2,0:T(8,128)} %copy-done.1), slice={[0:5], [0:64], [0:38], [0:134]} | slice | bytes 13035520 | tf_op jit(solution)/shard_map/slice | solution.py:101
  113.3 133.0 %while.11 = (s32[]{:T(128)}, f32[5,64,32,128]{3,2,1,0:T(8,128)}, f32[6,64,38,134]{3,2,1,0:T(8,128)}, f32[5,64,38,134]{3,1,2,0:T(8,128)}, f32[64,32,129]{2,1,0:T(...) while((s32[]{:T(128)}, f32[5,64,32,128]{3,2,1,0:T(8,128)}, f32[6,64,38,134]{3,2,1,0:T(8,128)}, ...), condition=%wide.region_1.2_spmd, body=%wide.region_0.1_spmd.sunk | while | flops 72130560 | bytes 36543056 | solution.py:97
  118.9 11.2 %multiply_add_fusion.9 = f32[64,32,129]{2,1,0:T(8,128)S(1)} fusion(f32[64,38,134]{2,1,0:T(8,128)S(1)} %get-tuple-element.196, f32[64,38,134]{2,1,0:T(8,128)S(1)} %get-tuple-element.197, f32[64,32,129]{2,1,0:T(8,128)S(1)} %get-tuple-element.216), kind=kLoop, calls=%fused_computation.4.clone.1 | loop fusion | flops 34873344 | bytes 10567680 | tf_op jit(solution)/shard_map/while/body/eval_jaxpr/add | solution.py:70
  130.1 7.9 multiply_add_fusion.8
  145.4 11.2 %multiply_add_fusion.9 = f32[64,32,129]{2,1,0:T(8,128)S(1)} fusion(f32[64,38,134]{2,1,0:T(8,128)S(1)} %get-tuple-element.196, f32[64,38,134]{2,1,0:T(8,128)S(1)} %get-tuple-element.197, f32[64,32,129]{2,1,0:T(8,128)S(1)} %get-tuple-element.216), kind=kLoop, calls=%fused_computation.4.clone.1 | loop fusion | flops 34873344 | bytes 10567680 | tf_op jit(solution)/shard_map/while/body/eval_jaxpr/add | solution.py:70
  156.6 7.9 multiply_add_fusion.8
  171.9 11.2 %multiply_add_fusion.9 = f32[64,32,129]{2,1,0:T(8,128)S(1)} fusion(f32[64,38,134]{2,1,0:T(8,128)S(1)} %get-tuple-element.196, f32[64,38,134]{2,1,0:T(8,128)S(1)} %get-tuple-element.197, f32[64,32,129]{2,1,0:T(8,128)S(1)} %get-tuple-element.216), kind=kLoop, calls=%fused_computation.4.clone.1 | loop fusion | flops 34873344 | bytes 10567680 | tf_op jit(solution)/shard_map/while/body/eval_jaxpr/add | solution.py:70
  183.1 7.9 multiply_add_fusion.8
  198.4 11.2 %multiply_add_fusion.9 = f32[64,32,129]{2,1,0:T(8,128)S(1)} fusion(f32[64,38,134]{2,1,0:T(8,128)S(1)} %get-tuple-element.196, f32[64,38,134]{2,1,0:T(8,128)S(1)} %get-tuple-element.197, f32[64,32,129]{2,1,0:T(8,128)S(1)} %get-tuple-element.216), kind=kLoop, calls=%fused_computation.4.clone.1 | loop fusion | flops 34873344 | bytes 10567680 | tf_op jit(solution)/shard_map/while/body/eval_jaxpr/add | solution.py:70
  209.6 7.9 multiply_add_fusion.8
  224.9 11.2 %multiply_add_fusion.9 = f32[64,32,129]{2,1,0:T(8,128)S(1)} fusion(f32[64,38,134]{2,1,0:T(8,128)S(1)} %get-tuple-element.196, f32[64,38,134]{2,1,0:T(8,128)S(1)} %get-tuple-element.197, f32[64,32,129]{2,1,0:T(8,128)S(1)} %get-tuple-element.216), kind=kLoop, calls=%fused_computation.4.clone.1 | loop fusion | flops 34873344 | bytes 10567680 | tf_op jit(solution)/shard_map/while/body/eval_jaxpr/add | solution.py:70
  236.1 7.9 multiply_add_fusion.8
  249.4 5.5 copy.114
  273.9 20.2 %all-to-all-start = ((f32[128,32,128]{2,1,0:T(8,128)}), f32[128,32,128]{2,1,0:T(8,128)S(1)}, u32[]{:S(2)}, u32[]{:S(2)}) async-start(f32[128,32,128]{2,1,0:T(8,128)} %bitcast.186), calls=%async_computation | async-start | bytes 4194304 | tf_op jit(solution)/shard_map/all_to_all | solution.py:231
  294.2 28.9 %all-to-all-done = f32[128,32,128]{2,1,0:T(8,128)S(1)} async-done(((f32[128,32,128]{2,1,0:T(8,128)}), f32[128,32,128]{2,1,0:T(8,128)S(1)}, u32[]{:S(2)}, u32[]{:S(2)}) %all-to-all-start) | async-done | bytes 2097184 | tf_op jit(solution)/shard_map/all_to_all | solution.py:231
  323.3 28.3 %fusion.84 = f32[4,1024,128]{1,2,0:T(8,128)S(1)} fusion(f32[4,1024,128]{2,1,0:T(8,128)S(1)} %bitcast.195, f32[1024]{0:T(1024)S(1)} %get-tuple-element.151, f32[1024]{0:T(1024)S(1)} %get-tuple-element.152), kind=kOutput, calls=%fused_computation.111 | convolution fusion | flops 6445596672 | bytes 4202496 | tf_op jit(solution)/shard_map/ky,pyx->pkx/dot_general | solution.py:247
  358.3 25.9 %all-to-all-done.1 = f32[4,1024,128]{2,0,1:T(4,128)S(1)} async-done(((f32[4,1024,128]{2,0,1:T(4,128)}), f32[4,1024,128]{2,0,1:T(4,128)S(1)}, u32[]{:S(2)}, u32[]{:S(2)}) %all-to-all-start.1) | async-done | bytes 2097184 | tf_op jit(solution)/shard_map/all_to_all | solution.py:235
  387.7 10.0 %fusion.118 = f32[4,256,512]{2,1,0:T(8,128)S(1)} fusion(f32[4,256,512]{1,2,0:T(8,128)S(1)} %bitcast.183, f32[512]{0:T(512)S(1)} %get-tuple-element.153, f32[512]{0:T(512)S(1)} %get-tuple-element.154), kind=kOutput, calls=%fused_computation.162 | convolution fusion | flops 3222011904 | bytes 4198400 | tf_op jit(solution)/shard_map/pyx,kx->pyk/dot_general | solution.py:252
  397.7 8.6 %fusion.69 = f32[4,256,512]{2,1,0:T(8,128)} fusion(f32[4,256,512]{2,1,0:T(8,128)S(1)} %fusion.118, f32[512]{0:T(512)S(1)} %multiply_subtract_fusion.5, f32[4,256]{1,0:T(4,128)S(1)} %broadcast_add_fusion, f32[512]{0:T(512)S(1)} %get-tuple-element.153, f32[512]{0:T(512)S(1)} %get-tuple-element.154), kind=kOutput, calls=%fused_computation.100 | convolution fusion | flops 3223060480 | bytes 4204544 | tf_op jit(solution)/shard_map/pyk,kx->pyx/dot_general | solution.py:259
  409.6 27.8 %all_to_all.54 = f32[4,1024,128]{2,0,1:T(4,128)S(1)} all-to-all(f32[4,1024,128]{2,0,1:T(4,128)S(1)} %bitcast.189), channel_id=1, replica_groups=mesh['rows'=4,'cols'=32] {'rows'}, dimensions={1} | all-to-all | bytes 4194304 | tf_op jit(solution)/shard_map/all_to_all | solution.py:235
  437.4 22.4 %fusion.87 = f32[4,1024,128]{1,2,0:T(8,128)} fusion(f32[1024]{0:T(1024)S(1)} %get-tuple-element.151, f32[1024]{0:T(1024)S(1)} %get-tuple-element.152, f32[4,1024,128]{2,0,1:T(4,128)S(1)} %all_to_all.54), kind=kOutput, calls=%fused_computation.112 | convolution fusion | flops 6445596672 | bytes 4202496 | tf_op jit(solution)/shard_map/ky,pkx->pyx/dot_general | solution.py:271
  474.2 22.3 %all-to-all-done.3 = f32[128,32,128]{2,1,0:T(8,128)S(1)} async-done(((f32[128,32,128]{2,1,0:T(8,128)}), f32[128,32,128]{2,1,0:T(8,128)S(1)}, u32[]{:S(2)}, u32[]{:S(2)}) %all-to-all-start.3) | async-done | bytes 2097184 | tf_op jit(solution)/shard_map/all_to_all | solution.py:231
  497.8 4.9 fusion.78
  522.1 4.7 pad_maximum_fusion.2
  526.8 123.6 %all-reduce.20.cloned.1.call-done = (f32[256]{0:T(256)}, f32[256,63]{0,1:T(8,128)}) async-done(((f32[256]{0:T(256)}, f32[256,63]{0,1:T(8,128)}), (f32[256]{0:T(256)}, f32[256,63]{0,1:T(8,128)})) %all-reduce.20.cloned.1.call-update) | async-done | bytes 65552 | tf_op jit(solution)/shard_map/psum | solution.py:313
  650.3 148.0 %all-reduce.18.cloned.1.call-done = f32[256,256]{1,0:T(8,128)} async-done(((f32[256,256]{1,0:T(8,128)}), f32[256,256]{1,0:T(8,128)}) %all-reduce.18.cloned.1.call-update) | async-done | bytes 262160 | tf_op jit(solution)/shard_map/psum | solution.py:313
  (172 shorter events, 155.2 us)
Async XLA Ops:
  7.2 249.5 %copy-start = (bf16[256,256]{1,0:T(8,128)(2,1)S(1)}, bf16[256,256]{1,0:T(8,128)(2,1)}, u32[]{:S(2)}) copy-start(bf16[256,256]{1,0:T(8,128)(2,1)} %param.13) | copy-start | bytes 393220
  7.9 7.4 copy-start.27
  8.9 6.5 copy-start.7
  15.4 6.1 copy-start.2
  26.0 10.2 %collective-permute-start = (f32[6,64,32,3]{1,2,3,0:T(8,128)S(1)}, f32[6,64,32,3]{1,2,3,0:T(8,128)S(1)}, u32[]{:S(2)}, u32[]{:S(2)}) collective-permute-start(f32[6,64,32,3]{1,2,3,0:T(8,128)S(1)} %copy.106), channel_id=1, source_target_pairs={{0,32},{32,64},{64,96},{1,33},{33,65},{65,97},{2,34},{34,66},{66,9... | collective-permute-start | bytes 442376 | tf_op jit(solution)/shard_map/ppermute | solution.py:24
  34.6 10.5 %collective-permute-start.1 = (f32[6,64,32,3]{1,2,3,0:T(8,128)S(1)}, f32[6,64,32,3]{1,2,3,0:T(8,128)S(1)}, u32[]{:S(2)}, u32[]{:S(2)}) collective-permute-start(f32[6,64,32,3]{1,2,3,0:T(8,128)S(1)} %copy.107), channel_id=1, source_target_pairs={{32,0},{64,32},{96,64},{33,1},{65,33},{97,65},{34,2},{66,34},{98,6... | collective-permute-start | bytes 442376 | tf_op jit(solution)/shard_map/ppermute | solution.py:27
  45.1 9.8 %slice-start = ((s8[5242880]{0:T(1024)(128)(4,1)}), s8[1048576]{0:T(1024)(128)(4,1)S(1)}, s32[]{:S(2)}) async-start(s8[5242880]{0:T(1024)(128)(4,1)} %bitcast.178), calls=%async_computation.6 | async-start | bytes 2097152
  49.2 5.7 slice-start.1
  52.2 7.9 collective-permute-start.2
  53.6 6.5 collective-permute-start.3
  56.4 4.9 copy-start.6
  70.8 5.3 copy-start.1
  77.9 31.4 %copy-start.9 = (f32[64,38,134]{2,0,1:T(8,128)}, f32[64,38,134]{2,0,1:T(8,128)S(1)}, u32[]{:S(2)}) copy-start(f32[64,38,134]{2,0,1:T(8,128)S(1)} %get-tuple-element.115) | copy-start | bytes 3910660
  254.9 7.9 copy-start.5
  258.0 2.3 copy-start.3
  262.8 2.3 copy-start.12
  262.8 2.7 copy-start.24
  262.9 3.0 copy-start.25
  264.9 2.2 copy-start.23
  273.9 49.1 %all-to-all-start = ((f32[128,32,128]{2,1,0:T(8,128)}), f32[128,32,128]{2,1,0:T(8,128)S(1)}, u32[]{:S(2)}, u32[]{:S(2)}) async-start(f32[128,32,128]{2,1,0:T(8,128)} %bitcast.186), calls=%async_computation | async-start | bytes 4194304 | tf_op jit(solution)/shard_map/all_to_all | solution.py:231
  353.4 30.9 %all-to-all-start.1 = ((f32[4,1024,128]{2,0,1:T(4,128)}), f32[4,1024,128]{2,0,1:T(4,128)S(1)}, u32[]{:S(2)}, u32[]{:S(2)}) async-start(f32[4,1024,128]{2,0,1:T(4,128)} %copy.129), calls=%async_computation.1 | async-start | bytes 4194304 | tf_op jit(solution)/shard_map/all_to_all | solution.py:235
  463.2 33.2 %all-to-all-start.3 = ((f32[128,32,128]{2,1,0:T(8,128)}), f32[128,32,128]{2,1,0:T(8,128)S(1)}, u32[]{:S(2)}, u32[]{:S(2)}) async-start(f32[128,32,128]{2,1,0:T(8,128)} %bitcast.184), calls=%async_computation.3 | async-start | bytes 4194304 | tf_op jit(solution)/shard_map/all_to_all | solution.py:231
  467.5 182.8 %all-reduce.20.cloned.1.call-start = ((), (), s32[]{:S(2)}) async-start(), calls=%async_computation.5 | async-start | bytes 133120 | tf_op jit(solution)/shard_map/psum | solution.py:313
  467.8 3.2 copy-start.18
  502.7 2.2 slice-start.2
  502.9 2.3 slice-start.3
  503.1 2.5 copy-start.20
  503.2 2.8 copy-start.21
  510.7 2.4 copy-start.4
  517.3 281.0 %all-reduce.18.cloned.1.call-start = ((), (), s32[]{:S(2)}) async-start(), calls=%async_computation.4 | async-start | bytes 524288 | tf_op jit(solution)/shard_map/psum | solution.py:313
  517.5 4.6 copy-start.15
  517.5 4.6 copy-start.19
  (12 other events, 16.7 us)
Sparse Core Ops, SparseCore 0:
  517.4 132.8 all-reduce.19
  655.7 142.6 all-reduce.17
where the time goes:
time: 820 us; the launch traced here: 810 us
  waiting for transfers between devices  354 us (43%)
  other arithmetic  151 us (18%)
  local copies, waits for them, and re-layouts  141 us (17%)
  matrix products  83.7 us (10%)
  starting transfers between devices  37.3 us (5%)
  blocking collectives  27.8 us (3%)
  between operations  14.9 us (2%)
    psum x2, waiting for transfers between devices, per_device(): lax.psum((grads[0], grads[1], grads[2]), ('rows', 'cols'))  272 us
    add x10, other arithmetic, flux_tendency(): jnp.maximum(face_speed, 0.0) * left_value  95.5 us
    all_to_all x2, waiting for transfers between devices, column_swap(): lax.all_to_all(block, 'cols', split_axis=0, concat_axis=1, tiled=True)  51.2 us
    dot_general x1, matrix products, horizontal_pencil(): gathered = jnp.einsum('ky,pyx->pkx', north_matrix, gathered, precision=high)  28.3 us
    all_to_all x1, blocking collectives, row_swap(): lax.all_to_all(block, 'rows', split_axis=1, concat_axis=2, tiled=True)  27.8 us
    while x4, local copies, waits for them, and re-layouts, advance(): lax.map(lambda tracer: advect_one(tracer, extended[0], extended[1], exten...  27.6 us
    all_to_all x1, waiting for transfers between devices, row_swap(): lax.all_to_all(block, 'rows', split_axis=1, concat_axis=2, tiled=True)  25.9 us
    all_to_all x2, starting transfers between devices, column_swap(): lax.all_to_all(block, 'cols', split_axis=0, concat_axis=1, tiled=True)  24.5 us
  transfers between devices with their start and end apart: 9, of which 7 were waited for; matrix products, arithmetic and copies ran while one was open for 4% of the time, Pallas kernels for 0%

commit v1 on v0

v1 whole, which is shorter than its diff:
```python
import functools
import math

import jax
import jax.numpy as jnp
import numpy as np
from jax import lax
from jax.experimental import pallas as pl
from jax.experimental.pallas import tpu as pltpu
from jax.sharding import PartitionSpec as P

NZ = 64
TIME_STEP = 0.2
SPECTRAL_SHIFT = 0.001
WENO_EPS = 1e-06
F32 = jnp.float32
BF16 = jnp.bfloat16
LANES = 128
NB = 32
ANY = pl.BlockSpec(memory_space=pl.ANY)
VM = pl.BlockSpec(memory_space=pltpu.VMEM)
MESH = pl.DeviceIdType.MESH


def dct_np(length):
    freq = np.arange(length)[:, None]
    cells = np.arange(length)[None, :]
    scale = np.where(freq == 0, np.sqrt(1.0 / length), np.sqrt(2.0 / length))
    return scale * np.cos(np.pi * (cells + 0.5) * freq / length)


def eigen_np(length):
    return 4.0 * np.sin(np.pi * np.arange(length) / (2 * length)) ** 2


def hi_lo_np(table):
    kind = np.dtype(BF16)
    hi = table.astype(np.float32).astype(kind)
    lo = (table - hi.astype(np.float64)).astype(np.float32).astype(kind)
    return jnp.asarray(hi), jnp.asarray(lo)


def level_tables(rows):
    base = dct_np(NZ)
    size = NZ // rows
    groups = [base[g * size : (g + 1) * size] for g in range(rows)]
    fwd = np.stack([np.concatenate([groups[(r + s) % rows] for s in range(rows)], 0) for r in range(rows)])
    inv = np.stack([np.concatenate([groups[(r - s) % rows] for s in range(rows)], 0).T for r in range(rows)])
    return hi_lo_np(fwd), hi_lo_np(inv)


def split(x):
    hi = x.astype(BF16)
    lo = (x - hi.astype(F32)).astype(BF16)
    return hi, lo


def dot3(a_hi, a_lo, b_hi, b_lo):
    dot = functools.partial(jnp.dot, preferred_element_type=F32)
    return dot(a_hi, b_hi) + (dot(a_hi, b_lo) + dot(a_lo, b_hi))


def dot_nt(a, b):
    return lax.dot_general(a, b, (((1,), (1,)), ((), ())), preferred_element_type=F32)


def level_ids(shape=(NZ, LANES)):
    return lax.broadcasted_iota(jnp.int32, shape, 0)


def above(x):
    return pltpu.roll(x, NZ - 1, 0)


def below(x):
    return pltpu.roll(x, 1, 0)


def dz(x, ids):
    up = jnp.where(ids == NZ - 1, 0.0, above(x))
    down = jnp.where(ids == 0, 0.0, below(x))
    return 0.5 * (up - down)


def depth_of(ocean, depth):
    return jnp.where(ocean == 1, depth, 0)


def pack_kernel(f_ref, ocean_ref, depth_ref, ft_ref, p_ref, lo_ref, hi_ref):
    f = pl.program_id(0)
    ids = level_ids()
    lane = lax.broadcasted_iota(jnp.int32, (NZ, LANES), 1)
    depth = depth_of(ocean_ref[...], depth_ref[...])

    def slot_mask(lanes, slot):
        rel = lax.rem(lanes - 8 * slot + 3 + LANES, LANES)
        return rel < 6

    for g in range(NB // 16):
        packed = jnp.zeros((NZ, LANES), F32)
        packed_d = jnp.zeros((8, LANES), F32)
        lane8 = lax.broadcasted_iota(jnp.int32, (8, LANES), 1)
        for yi in range(16):
            y = g * 16 + yi
            row = depth[y : y + 1, :]
            q = jnp.where(ids < row, f_ref[0, pl.ds(y, NZ, stride=NB), :], 0.0)
            ft_ref[0, y] = q
            moved = pltpu.roll(q, 8 * yi, 1) if yi else q
            packed = jnp.where(slot_mask(lane, yi), moved, packed)
            d8 = jnp.broadcast_to(row.astype(F32), (8, LANES))
            moved_d = pltpu.roll(d8, 8 * yi, 1) if yi else d8
            packed_d = jnp.where(slot_mask(lane8, yi), moved_d, packed_d)
            if y < 3:
                lo_ref[pl.ds(pl.multiple_of((f * 3 + y) * NZ, NZ), NZ), :] = q
            if y >= NB - 3:
                hi_ref[pl.ds(pl.multiple_of((f * 3 + y - (NB - 3)) * NZ, NZ), NZ), :] = q
        p_ref[pl.ds(pl.multiple_of((f * 2 + g) * NZ, NZ), NZ), :] = packed
        p_ref[pl.ds(640 + g * 8, 8), :] = packed_d
    lo_ref[pl.ds(960, 8), :] = jnp.broadcast_to(depth[0:1].astype(F32), (8, LANES))
    hi_ref[pl.ds(960, 8), :] = jnp.broadcast_to(depth[NB - 1 : NB].astype(F32), (8, LANES))


def pack(fields, ocean, depth):
    full = lambda shape: pl.BlockSpec(shape, lambda f: (0,) * len(shape))
    return pl.pallas_call(
        pack_kernel,
        grid=(5,),
        in_specs=[
            pl.BlockSpec((1, NZ * NB, LANES), lambda f: (f, 0, 0)),
            full((NB, LANES)),
            full((NB, LANES)),
        ],
        out_specs=[
            pl.BlockSpec((1, NB, NZ, LANES), lambda f: (f, 0, 0, 0)),
            full((656, LANES)),
            full((968, LANES)),
            full((968, LANES)),
        ],
        out_shape=[
            jax.ShapeDtypeStruct((5, NB, NZ, LANES), F32),
            jax.ShapeDtypeStruct((656, LANES), F32),
            jax.ShapeDtypeStruct((968, LANES), F32),
            jax.ShapeDtypeStruct((968, LANES), F32),
        ],
        cost_estimate=pl.CostEstimate(flops=10_000_000, bytes_accessed=12_000_000, transcendentals=0),
        name="pack",
    )(fields.reshape(5, NZ * NB, LANES), ocean, depth)


def adjoint_kernel(rows, c_ref, ocean_ref, depth_ref, fh_ref, fl_ref, *outs):
    src = outs[rows]
    r = lax.axis_index("rows")
    ids = level_ids()
    depth = depth_of(ocean_ref[...], depth_ref[...])
    for half in range(4):
        for yi in range(8):
            y = half * 8 + yi
            w = jnp.where(ids < depth[y : y + 1, :], c_ref[0, pl.ds(y, NZ, stride=NB), :], 0.0)
            src[:, yi * LANES : (yi + 1) * LANES] = TIME_STEP * dz(w, ids)
        hi, lo = split(src[...])
        res = dot3(fh_ref[r], fl_ref[r], hi, lo)
        size = NZ // rows
        for s in range(rows):
            for yi in range(8):
                outs[s][half * 8 + yi] = res[s * size : (s + 1) * size, yi * LANES : (yi + 1) * LANES]


def adjoint_source(cotangent, ocean, depth, fwd, rows):
    size = NZ // rows
    return pl.pallas_call(
        functools.partial(adjoint_kernel, rows),
        grid=(1,),
        in_specs=[
            pl.BlockSpec((1, NZ * NB, LANES), lambda i: (2, 0, 0)),
            pl.BlockSpec((NB, LANES), lambda i: (0, 0)),
            pl.BlockSpec((NB, LANES), lambda i: (0, 0)),
            pl.BlockSpec((rows, NZ, NZ), lambda i: (0, 0, 0)),
            pl.BlockSpec((rows, NZ, NZ), lambda i: (0, 0, 0)),
        ],
        out_specs=[pl.BlockSpec((NB, size, LANES), lambda i: (0, 0, 0))] * rows,
        out_shape=[jax.ShapeDtypeStruct((NB, size, LANES), F32)] * rows,
        scratch_shapes=[pltpu.VMEM((NZ, 8 * LANES), F32)],
        cost_estimate=pl.CostEstimate(flops=10_000_000, bytes_accessed=2_100_000, transcendentals=0),
        name="adjoint",
    )(cotangent.reshape(5, NZ * NB, LANES), ocean, depth, *fwd)


def corrected(pos, speed, mag, y1, y2, y3, y4, y5, qm, qp):
    x1 = jnp.where(pos, y1, y5)
    x2 = jnp.where(pos, y2, y4)
    x3 = y3
    x4 = jnp.where(pos, y4, y2)
    c = jnp.where(pos, qm, qp)
    d1 = x2 - x1
    d2 = x3 - x2
    d3 = x4 - x3
    x3d = x3 + x3
    t0 = d1 + (x2 + x2)
    t1 = x2 + x3
    t2 = d3 - x3d
    eps4 = 4.0 * WENO_EPS
    e0 = (eps4 + t0 * t0) + (13.0 / 3.0) * (d1 * d1)
    e1 = (eps4 + t1 * t1) + (13.0 / 3.0) * (d2 * d2)
    e2 = (eps4 + t2 * t2) + (13.0 / 3.0) * (d3 * d3)
    f0 = e1 * e2
    f1 = e0 * e2
    f2 = e0 * e1
    g0 = f0 * f0
    g1 = 6.0 * (f1 * f1)
    g2 = 3.0 * (f2 * f2)
    k0 = t0 + d1 + x2
    k1 = t1 + x3
    k2 = x3d - d3 + x3
    num = g0 * k0 + g1 * k1 + g2 * k2
    den = g0 + g1 + g2
    return speed * c + mag * (num / den)


def advect_kernel(ft_ref, own_ref, east_ref, west_ref, south_ref, north_ref, depth_ref, ocean_ref,
                  adv_ref, spread_ref, ext, dext, exy, fxe, edge_d):
    zb = pl.program_id(0)
    z0 = pl.multiple_of(zb * 8, 8)
    zf = (lax.broadcasted_iota(jnp.int32, (8, LANES), 0) + z0).astype(F32)
    lane = lax.broadcasted_iota(jnp.int32, (8, LANES), 1)
    in_hi = lax.rem(lane, 8) < 4
    first, second = lane == 0, lane <= 1
    last, last2 = lane == LANES - 1, lane >= LANES - 2

    depth = depth_of(ocean_ref[...], depth_ref[...]).astype(F32)
    dext[8:40] = depth
    dext[7:8] = south_ref[960:961]
    dext[40:41] = north_ref[960:961]
    for f in range(5):
        for r in range(3):
            at = pl.ds(pl.multiple_of((f * 3 + r) * NZ + z0, 8), 8)
            ext[f, r] = south_ref[at]
            ext[f, 3 + NB + r] = north_ref[at]
        ext[f, 3 : 3 + NB] = ft_ref[f]

    for g in range(2):
        at_d = pl.ds(640 + g * 8, 8)
        edge_d[g] = jnp.where(in_hi, east_ref[at_d], west_ref[at_d])
        d_face = jnp.where(in_hi, east_ref[at_d], own_ref[at_d])
        d_face = jnp.minimum(d_face, pltpu.roll(d_face, 1, 1))
        for f in range(5):
            at = pl.ds(pl.multiple_of((f * 2 + g) * NZ + z0, 8), 8)
            exy[f, g] = jnp.where(in_hi, east_ref[at], west_ref[at])
            q = jnp.where(in_hi, east_ref[at], own_ref[at])
            qm = pltpu.roll(q, 1, 1)
            if f == 0:
                speed = jnp.where(zf < d_face, 0.5 * (q + qm), 0.0)
                pos = speed > 0
                mag = jnp.abs(speed) * (1.0 / 6.0)
            d = q - qm
            fxe[f, g] = corrected(
                pos, speed, mag, pltpu.roll(d, 2, 1), pltpu.roll(d, 1, 1), d,
                pltpu.roll(d, LANES - 1, 1), pltpu.roll(d, LANES - 2, 1), qm, q,
            )

    def face_y(j):
        d_face = jnp.minimum(dext[pl.ds(j + 7, 1), :], dext[pl.ds(j + 8, 1), :])
        out = []
        v = [ext[1, j + 2], ext[1, j + 3]]
        speed = jnp.where(zf < d_face, 0.5 * (v[0] + v[1]), 0.0)
        pos = speed > 0
        mag = jnp.abs(speed) * (1.0 / 6.0)
        dv = None
        for f in range(5):
            q = [ext[f, j + o] for o in range(6)]
            d = [q[o + 1] - q[o] for o in range(5)]
            if f == 1:
                dv = d[2]
            out.append(corrected(pos, speed, mag, d[0], d[1], d[2], d[3], d[4], q[2], q[3]))
        return out, dv

    def step(j, carry):
        below_flux, below_dv = carry
        above_flux, above_dv = face_y(j + 1)
        g = j // 16
        yi = lax.rem(j, 16)
        back = lax.rem(LANES - 8 * yi, LANES)
        to_last = LANES - 1 - 8 * yi
        drow = dext[pl.ds(j + 8, 1), :]
        d8 = jnp.broadcast_to(drow, (8, LANES))
        ed = pltpu.roll(edge_d[g], back, 1)
        d_face = jnp.minimum(d8, pltpu.roll(jnp.where(last, ed, d8), 1, 1))
        wet = zf < d8
        du = None
        for f in range(5):
            q = ext[f, j + 3]
            e = pltpu.roll(exy[f, g], back, 1)
            qm = pltpu.roll(jnp.where(last, e, q), 1, 1)
            em = pltpu.roll(jnp.where(last, q, e), 1, 1)
            d = q - qm
            de = e - em
            if f == 0:
                speed = jnp.where(zf < d_face, 0.5 * (q + qm), 0.0)
                pos = speed > 0
                mag = jnp.abs(speed) * (1.0 / 6.0)
            y1 = pltpu.roll(jnp.where(last2, de, d), 2, 1)
            y2 = pltpu.roll(jnp.where(last, de, d), 1, 1)
            y4 = pltpu.roll(jnp.where(first, de, d), LANES - 1, 1)
            y5 = pltpu.roll(jnp.where(second, de, d), LANES - 2, 1)
            if f == 0:
                du = d + y4
            flux = corrected(pos, speed, mag, y1, y2, d, y4, y5, qm, q)
            east = jnp.where(last, pltpu.roll(fxe[f, g], to_last, 1), pltpu.roll(flux, LANES - 1, 1))
            total = (flux - east) + (below_flux[f] - above_flux[f])
            adv_ref[f, j] = jnp.where(wet, q + TIME_STEP * total, 0.0)
        spread_ref[j] = 0.5 * du + 0.5 * (below_dv + above_dv)
        return above_flux, above_dv

    lax.fori_loop(0, NB, step, face_y(0))


def advect(ft, own, east, west, south, north, depth, ocean):
    full = lambda shape: pl.BlockSpec(shape, lambda i: (0,) * len(shape))
    return pl.pallas_call(
        advect_kernel,
        grid=(NZ // 8,),
        in_specs=[
            pl.BlockSpec((5, NB, 8, LANES), lambda i: (0, 0, i, 0)),
            full((656, LANES)), full((656, LANES)), full((656, LANES)),
            full((968, LANES)), full((968, LANES)),
            full((NB, LANES)), full((NB, LANES)),
        ],
        out_specs=[
            pl.BlockSpec((5, NB, 8, LANES), lambda i: (0, 0, i, 0)),
            pl.BlockSpec((NB, 8, LANES), lambda i: (0, i, 0)),
        ],
        out_shape=[
            jax.ShapeDtypeStruct((5, NB, NZ, LANES), F32),
            jax.ShapeDtypeStruct((NB, NZ, LANES), F32),
        ],
        scratch_shapes=[
            pltpu.VMEM((5, NB + 6, 8, LANES), F32),
            pltpu.VMEM((48, LANES), F32),
            pltpu.VMEM((5, 2, 8, LANES), F32),
            pltpu.VMEM((5, 2, 8, LANES), F32),
            pltpu.VMEM((2, 8, LANES), F32),
        ],
        cost_estimate=pl.CostEstimate(flops=200_000_000, bytes_accessed=130_000_000, transcendentals=0),
        name="advect",
    )(ft, own, east, west, south, north, depth, ocean)


def forward_kernel(rows, adv_ref, w_ref, spread_ref, depth_ref, ocean_ref, win_ref, bin_ref, wout_ref,
                   fh_ref, fl_ref, *refs):
    pieces = refs[:rows]
    rates_ref, act_ref, hs_ref, feats, rate_s, src = refs[rows:]
    r = lax.axis_index("rows")
    ids = level_ids()
    depth = depth_of(ocean_ref[...], depth_ref[...])
    for n, f in enumerate((0, 1, 3, 4)):
        for yi in range(8):
            feats[n * NZ : (n + 1) * NZ, yi * LANES : (yi + 1) * LANES] = adv_ref[f, yi].astype(BF16)
    pre = lax.dot_general(win_ref[...], feats[...], (((0,), (0,)), ((), ())), preferred_element_type=F32)
    act = jnp.tanh(pre + bin_ref[...])
    act_ref[0] = act
    out = lax.dot_general(wout_ref[...], act.astype(BF16), (((0,), (0,)), ((), ())), preferred_element_type=F32)
    rate_s[...] = 2.0 * jax.nn.sigmoid(out)
    for yi in range(8):
        cols = slice(yi * LANES, (yi + 1) * LANES)
        row = depth[yi : yi + 1, :]
        wet = ids < row
        rates = rate_s[:, cols]
        rates_ref[yi] = rates
        mixed = []
        for n, f in enumerate((3, 4)):
            t = adv_ref[f, yi]
            flux = jnp.where(ids + 1 < row, rates * (above(t) - t), 0.0)
            m = jnp.where(wet, t + TIME_STEP * (flux - below(flux)), 0.0)
            hs_ref[n, yi] = m
            mixed.append(m)
        density = 0.5 * mixed[0] - 0.5 * mixed[1]
        rhs = dz(density, ids) - (spread_ref[yi] + dz(w_ref[0, yi], ids)) / TIME_STEP
        src[:, cols] = jnp.where(wet, rhs, 0.0)
    hi, lo = split(src[...])
    res = dot3(fh_ref[r], fl_ref[r], hi, lo)
    size = NZ // rows
    for s in range(rows):
        for yi in range(8):
            pieces[s][yi] = res[s * size : (s + 1) * size, yi * LANES : (yi + 1) * LANES]


def closure_forward(adv, ft, spread, depth, ocean, win, b_in, wout, fwd, rows):
    size = NZ // rows
    full = lambda shape: pl.BlockSpec(shape, lambda i: (0,) * len(shape))
    plane = pl.BlockSpec((8, LANES), lambda i: (i, 0))
    ycol = pl.BlockSpec((8, NZ, LANES), lambda i: (i, 0, 0))
    return pl.pallas_call(
        functools.partial(forward_kernel, rows),
        grid=(NB // 8,),
        in_specs=[
            pl.BlockSpec((5, 8, NZ, LANES), lambda i: (0, i, 0, 0)),
            pl.BlockSpec((1, 8, NZ, LANES), lambda i: (2, i, 0, 0)),
            ycol, plane, plane,
            full((256, 256)), full((256, 1)), full((256, NZ)),
            full((rows, NZ, NZ)), full((rows, NZ, NZ)),
        ],
        out_specs=[pl.BlockSpec((8, size, LANES), lambda i: (i, 0, 0))] * rows
        + [ycol, pl.BlockSpec((1, 256, 1024), lambda i: (i, 0, 0)),
           pl.BlockSpec((2, 8, NZ, LANES), lambda i: (0, i, 0, 0))],
        out_shape=[jax.ShapeDtypeStruct((NB, size, LANES), F32)] * rows
        + [
            jax.ShapeDtypeStruct((NB, NZ, LANES), F32),
            jax.ShapeDtypeStruct((NB // 8, 256, 1024), F32),
            jax.ShapeDtypeStruct((2, NB, NZ, LANES), F32),
        ],
        scratch_shapes=[
            pltpu.VMEM((256, 1024), BF16),
            pltpu.VMEM((NZ, 1024), F32),
            pltpu.VMEM((NZ, 1024), F32),
        ],
        cost_estimate=pl.CostEstimate(flops=900_000_000, bytes_accessed=18_000_000, transcendentals=1_500_000),
        name="closure_forward",
    )(adv, ft, spread, depth, ocean, win, b_in, wout, *fwd)


def root_of(d):
    q = jnp.sqrt(d + 0.25 * d * d)
    return 1.0 / (1.0 + 0.5 * d + q), 0.5 / q


def exchange_rows(rows, cols, chunk):
    n = NZ // cols
    tile = max(8, 2 * n)
    start = (chunk // n) * tile + chunk % n
    return start, (rows // n) * tile, n, tile


def line_kernel(rows, cols, *refs):
    pieces = refs[:rows]
    ch_ref, cl_ref, lv_ref, ex_ref, v_ref, s_ref, work = refs[rows:]
    r = lax.axis_index("rows")
    size = NZ // rows
    wide = rows * LANES
    total = None
    for s in range(rows):
        src = lax.rem(r - s + rows, rows)
        at = pl.ds(pl.multiple_of(src * LANES, LANES), LANES)
        hi, lo = split(pieces[s][...])
        part = dot3(hi, lo, ch_ref[at, :], cl_ref[at, :])
        total = part if total is None else total + part
    work[...] = total
    d = lv_ref[pl.ds(pl.multiple_of(r * size, size), size), :] + ex_ref[...]
    lam, _ = root_of(d)

    def causal(y, c):
        at = pl.ds(pl.multiple_of(y * size, size), size)
        c = work[at] + lam * c
        v_ref[at] = c
        return c

    end = lax.fori_loop(0, NB, causal, jnp.zeros((size, wide), F32))

    def anticausal(i, a):
        at = pl.ds(pl.multiple_of((NB - 1 - i) * size, size), size)
        x = work[at]
        v_ref[at] = v_ref[at] + lam * a
        return x + lam * a

    start = lax.fori_loop(0, NB, anticausal, jnp.zeros((size, wide), F32))
    s_ref[...] = jnp.zeros_like(s_ref)
    for ch in range(rows):
        row, stride, n, _ = exchange_rows(rows, cols, ch)
        lanes = slice(ch * LANES, (ch + 1) * LANES)
        s_ref[pl.ds(row, size, stride=stride), :] = start[:, lanes]
        s_ref[pl.ds(row + n, size, stride=stride), :] = end[:, lanes]


def line_solve(pieces, tables, rows, cols):
    size = NZ // rows
    wide = rows * LANES
    tile = exchange_rows(rows, cols, 0)[3]
    return pl.pallas_call(
        functools.partial(line_kernel, rows, cols),
        in_specs=[VM] * (rows + 4),
        out_specs=[VM, VM],
        out_shape=[
            jax.ShapeDtypeStruct((NB * size, wide), F32),
            jax.ShapeDtypeStruct((cols * tile, LANES), F32),
        ],
        scratch_shapes=[pltpu.VMEM((NB * size, wide), F32)],
        cost_estimate=pl.CostEstimate(flops=800_000_000, bytes_accessed=4_500_000, transcendentals=0),
        name="line_solve",
    )(*[p.reshape(NB * size, LANES) for p in pieces], *tables)


def carry_kernel(rows, cols, s_ref, lv_ref, ex_ref, c_ref, got, send, dsem, send_sem, recv_sem, send2_sem, recv2_sem):
    n = NZ // cols
    tile = max(8, 2 * n)
    me = lax.axis_index("cols")
    r = lax.axis_index("rows")
    barrier = pltpu.get_barrier_semaphore()

    def greet(t, carry):
        pl.semaphore_signal(barrier, inc=1, device_id={"cols": lax.rem(me + t, cols)}, device_id_type=MESH)
        return carry

    lax.fori_loop(1, cols, greet, 0)
    pl.semaphore_wait(barrier, cols - 1)

    def out_copy(t):
        peer = lax.rem(me + t, cols)
        return pltpu.make_async_remote_copy(
            src_ref=s_ref.at[peer], dst_ref=got.at[me], send_sem=send_sem.at[t], recv_sem=recv_sem.at[t],
            device_id={"cols": peer}, device_id_type=MESH,
        )

    def back_copy(t):
        peer = lax.rem(me + t, cols)
        return pltpu.make_async_remote_copy(
            src_ref=send.at[peer], dst_ref=c_ref.at[me], send_sem=send2_sem.at[t], recv_sem=recv2_sem.at[t],
            device_id={"cols": peer}, device_id_type=MESH,
        )

    def run(make):
        lax.fori_loop(1, cols, lambda t, c: (make(t).start(), c)[1], 0)

    def finish(make):
        lax.fori_loop(1, cols, lambda t, c: (make(t).wait(), c)[1], 0)

    run(out_copy)
    mine = pltpu.make_async_copy(s_ref.at[me], got.at[me], dsem.at[0])
    mine.start()
    size = NZ // rows
    level = r * size + (me * n) // rows
    chunk = lax.rem(me, rows // n)
    lam, _ = root_of(lv_ref[level] + ex_ref[chunk])
    mu = lam
    for _ in range(NB.bit_length() - 1):
        mu = mu * mu
    whole = mu
    for _ in range(cols.bit_length() - 1):
        whole = whole * whole
    scale = 1.0 / (1.0 - whole * whole)
    is_start = lax.broadcasted_iota(jnp.int32, (tile, LANES), 0) < n
    mine.wait()
    finish(out_copy)

    zero = jnp.zeros((tile, LANES), F32)
    sa = lax.fori_loop(0, cols, lambda k, a: got[cols - 1 - k] + mu * a, zero)
    sb = lax.fori_loop(0, cols, lambda k, b: got[k] + mu * b, zero)
    left = (pltpu.roll(sa, n, 0) + whole * sb) * scale
    right = (pltpu.roll(sb, tile - n, 0) + whole * sa) * scale

    def ascend(k, c):
        send[k] = c
        return got[k] + mu * c

    lax.fori_loop(0, cols, ascend, left)

    def descend(i, c):
        k = cols - 1 - i
        send[k] = jnp.where(is_start, c, send[k])
        return got[k] + mu * c

    lax.fori_loop(0, cols, descend, right)
    run(back_copy)
    mine2 = pltpu.make_async_copy(send.at[me], c_ref.at[me], dsem.at[1])
    mine2.start()
    mine2.wait()
    finish(back_copy)


def carries(moments, rows, cols, cid):
    _, _, n, tile = exchange_rows(rows, cols, 0)
    level_list = jnp.asarray(SPECTRAL_SHIFT + eigen_np(NZ), F32)
    east = eigen_np(rows * LANES).reshape(rows // n, n, LANES)
    east_tiles = jnp.asarray(east[:, np.arange(tile) % n], F32)
    return pl.pallas_call(
        functools.partial(carry_kernel, rows, cols),
        in_specs=[VM, pl.BlockSpec(memory_space=pltpu.SMEM), VM],
        out_specs=VM,
        out_shape=jax.ShapeDtypeStruct((cols, tile, LANES), F32),
        scratch_shapes=[
            pltpu.VMEM((cols, tile, LANES), F32),
            pltpu.VMEM((cols, tile, LANES), F32),
            pltpu.SemaphoreType.DMA((2,)),
            pltpu.SemaphoreType.DMA((cols,)),
            pltpu.SemaphoreType.DMA((cols,)),
            pltpu.SemaphoreType.DMA((cols,)),
            pltpu.SemaphoreType.DMA((cols,)),
        ],
        compiler_params=pltpu.CompilerParams(collective_id=cid, has_side_effects=True),
        name="carries",
    )(moments.reshape(cols, tile, LANES), level_list, east_tiles)


def back_kernel(rows, cols, v_ref, c_ref, ch_ref, cl_ref, lv_ref, ex_ref, *refs):
    outs = refs[:rows]
    work = refs[rows]
    r = lax.axis_index("rows")
    size = NZ // rows
    d = lv_ref[pl.ds(pl.multiple_of(r * size, size), size), :] + ex_ref[...]
    lam, kappa = root_of(d)
    left, right = [], []
    for ch in range(rows):
        row, stride, n, _ = exchange_rows(rows, cols, ch)
        right.append(c_ref[pl.ds(row, size, stride=stride), :])
        left.append(c_ref[pl.ds(row + n, size, stride=stride), :])
    left = jnp.concatenate(left, 1) * (lam * kappa)
    right = jnp.concatenate(right, 1) * (lam * kappa)

    def fwd(y, h):
        at = pl.ds(pl.multiple_of(y * size, size), size)
        work[at] = kappa * v_ref[at] + h
        return lam * h

    lax.fori_loop(0, NB, fwd, left)

    def bwd(i, h):
        at = pl.ds(pl.multiple_of((NB - 1 - i) * size, size), size)
        work[at] = work[at] + h
        return lam * h

    lax.fori_loop(0, NB, bwd, right)
    hi, lo = split(work[...])
    for s in range(rows):
        dst = lax.rem(r + s, rows)
        outs[s][...] = dot3(hi, lo, ch_ref[dst], cl_ref[dst])


def line_back(v, c, tables, rows, cols):
    size = NZ // rows
    outs = pl.pallas_call(
        functools.partial(back_kernel, rows, cols),
        in_specs=[VM] * 6,
        out_specs=[VM] * rows,
        out_shape=[jax.ShapeDtypeStruct((NB * size, LANES), F32)] * rows,
        scratch_shapes=[pltpu.VMEM((NB * size, rows * LANES), F32)],
        cost_estimate=pl.CostEstimate(flops=800_000_000, bytes_accessed=4_500_000, transcendentals=0),
        name="line_back",
    )(v, c.reshape(-1, LANES), *tables)
    return [o.reshape(NB, size, LANES) for o in outs]


def gather_levels(pieces, rows, buf, base=0):
    size = NZ // rows
    for s in range(rows):
        for yi in range(8):
            buf[s * size : (s + 1) * size, yi * LANES : (yi + 1) * LANES] = pieces[s][base + yi]


def backward_kernel(rows, *refs):
    pieces = refs[:rows]
    (adv_ref, ct_ref, cs_ref, rates_ref, act_ref, depth_ref, ocean_ref, wout_ref, ih_ref, il_ref,
     g_ref, buf, feats, gos, gw, gwo, gb) = refs[rows:]
    i = pl.program_id(0)
    r = lax.axis_index("rows")
    ids = level_ids()
    depth = depth_of(ocean_ref[...], depth_ref[...])
    gather_levels(pieces, rows, buf)
    hi, lo = split(buf[...])
    buf[...] = dot3(ih_ref[r], il_ref[r], hi, lo)
    for n, f in enumerate((0, 1, 3, 4)):
        for yi in range(8):
            feats[n * NZ : (n + 1) * NZ, yi * LANES : (yi + 1) * LANES] = adv_ref[f, yi].astype(BF16)
    for yi in range(8):
        cols = slice(yi * LANES, (yi + 1) * LANES)
        row = depth[yi : yi + 1, :]
        wet = ids < row
        grad_density = -dz(jnp.where(wet, buf[:, cols], 0.0), ids)
        rates = rates_ref[yi]
        total = None
        for f, c_ref, sign in ((3, ct_ref, 0.5), (4, cs_ref, -0.5)):
            grad = c_ref[0, pl.ds(yi, NZ, stride=8), :] + sign * grad_density
            grad = jnp.where(wet, grad, 0.0)
            t = adv_ref[f, yi]
            term = (grad - above(grad)) * (above(t) - t)
            total = term if total is None else total + term
        grad_rates = jnp.where(ids + 1 < row, TIME_STEP * total, 0.0)
        gos[:, cols] = (grad_rates * rates * (1.0 - 0.5 * rates)).astype(BF16)
    act = act_ref[0]
    go = gos[...]
    gpre = jnp.dot(wout_ref[...], go, preferred_element_type=F32) * (1.0 - act * act)
    p_hi, p_lo = split(gpre)
    ones = jnp.ones((8, 1024), BF16)

    @pl.when(i == 0)
    def _():
        gw[...] = jnp.zeros_like(gw)
        gwo[...] = jnp.zeros_like(gwo)
        gb[...] = jnp.zeros_like(gb)

    gw[...] += dot_nt(feats[...], p_hi)
    gwo[...] += dot_nt(go, act.astype(BF16))
    gb[...] += dot_nt(ones, p_hi) + dot_nt(ones, p_lo)

    @pl.when(i == NB // 8 - 1)
    def _():
        for h in range(2):
            lanes = slice(h * LANES, (h + 1) * LANES)
            g_ref[h * 256 : (h + 1) * 256] = gw[:, lanes]
            g_ref[512 + h * NZ : 512 + (h + 1) * NZ] = gwo[:, lanes]
            g_ref[575 + h * NZ : 576 + h * NZ] = gb[0:1, lanes]
        g_ref[640:1024] = jnp.zeros((384, LANES), F32)


def closure_backward(pieces, adv, cotangent, rates, act, depth, ocean, wout, inv, rows):
    size = NZ // rows
    full = lambda shape: pl.BlockSpec(shape, lambda i: (0,) * len(shape))
    plane = pl.BlockSpec((8, LANES), lambda i: (i, 0))
    ycol = pl.BlockSpec((8, NZ, LANES), lambda i: (i, 0, 0))
    cot = cotangent.reshape(5, NZ, NB // 8, 8, LANES)

    def kernel(*refs):
        refs = list(refs)
        for at in (rows + 1, rows + 2):
            refs[at] = refs[at].reshape(1, NZ * 8, LANES)
        backward_kernel(rows, *refs)

    cot_spec = lambda f: pl.BlockSpec((1, NZ, 1, 8, LANES), lambda i: (f, 0, i, 0, 0))
    return pl.pallas_call(
        kernel,
        grid=(NB // 8,),
        in_specs=[pl.BlockSpec((8, size, LANES), lambda i: (i, 0, 0))] * rows
        + [
            pl.BlockSpec((5, 8, NZ, LANES), lambda i: (0, i, 0, 0)),
            cot_spec(3), cot_spec(4), ycol,
            pl.BlockSpec((1, 256, 1024), lambda i: (i, 0, 0)),
            plane, plane, full((256, NZ)), full((rows, NZ, NZ)), full((rows, NZ, NZ)),
        ],
        out_specs=full((1024, LANES)),
        out_shape=jax.ShapeDtypeStruct((1024, LANES), F32),
        scratch_shapes=[
            pltpu.VMEM((NZ, 1024), F32),
            pltpu.VMEM((256, 1024), BF16),
            pltpu.VMEM((NZ, 1024), BF16),
            pltpu.VMEM((256, 256), F32),
            pltpu.VMEM((NZ, 256), F32),
            pltpu.VMEM((8, 256), F32),
        ],
        cost_estimate=pl.CostEstimate(flops=1_200_000_000, bytes_accessed=16_000_000, transcendentals=0),
        name="closure_backward",
    )(*pieces, adv, cot, cot, rates, act, depth, ocean, wout, *inv)


def sum_kernel(rows, cols, g_ref, o_ref, land, acc, land2, total, dsem, s1, r1, s2, r2, s3, r3, s4, r4):
    me = lax.axis_index("cols")
    r = lax.axis_index("rows")
    barrier = pltpu.get_barrier_semaphore()

    def greet(t, carry):
        pl.semaphore_signal(barrier, inc=1, device_id={"cols": lax.rem(me + t, cols)}, device_id_type=MESH)
        return carry

    lax.fori_loop(1, cols, greet, 0)
    for t in range(1, rows):
        pl.semaphore_signal(barrier, inc=1, device_id={"rows": lax.rem(r + t, rows)}, device_id_type=MESH)
    pl.semaphore_wait(barrier, cols - 1 + rows - 1)

    def copy(axis, count, at, t, src, dst, ss, rs):
        return pltpu.make_async_remote_copy(
            src_ref=src, dst_ref=dst, send_sem=ss.at[t], recv_sem=rs.at[t],
            device_id={axis: lax.rem(at + t, count)}, device_id_type=MESH,
        )

    def rows_out(t):
        return copy("rows", rows, r, t, g_ref.at[lax.rem(r + t, rows)], land.at[t], s1, r1)

    def cols_out(t):
        return copy("cols", cols, me, t, acc.at[lax.rem(me + t, cols)], land2.at[t], s2, r2)

    def cols_back(t):
        return copy("cols", cols, me, t, total.at[me], total.at[me], s3, r3)

    def rows_back(t):
        return copy("rows", rows, r, t, total, o_ref.at[r], s4, r4)

    def all_of(make, count):
        lax.fori_loop(1, count, lambda t, c: (make(t).start(), c)[1], 0)
        lax.fori_loop(1, count, lambda t, c: (make(t).wait(), c)[1], 0)

    all_of(rows_out, rows)
    value = g_ref[r]
    for t in range(1, rows):
        value = value + land[t]
    acc[...] = value
    all_of(cols_out, cols)
    tile = lax.fori_loop(1, cols, lambda t, v: v + land2[t], acc[me])
    total[me] = tile
    all_of(cols_back, cols)
    own = pltpu.make_async_copy(total, o_ref.at[r], dsem.at[0])
    own.start()
    all_of(rows_back, rows)
    own.wait()


def sum_gradients(g, rows, cols, cid):
    tile = 1024 // (rows * cols)
    sems = []
    for count in (rows, cols, cols, rows):
        sems += [pltpu.SemaphoreType.DMA((count,)), pltpu.SemaphoreType.DMA((count,))]
    return pl.pallas_call(
        functools.partial(sum_kernel, rows, cols),
        in_specs=[VM],
        out_specs=VM,
        out_shape=jax.ShapeDtypeStruct((rows, cols, tile, LANES), F32),
        scratch_shapes=[
            pltpu.VMEM((rows, cols, tile, LANES), F32),
            pltpu.VMEM((cols, tile, LANES), F32),
            pltpu.VMEM((cols, tile, LANES), F32),
            pltpu.VMEM((cols, tile, LANES), F32),
            pltpu.SemaphoreType.DMA((1,)),
            *sems,
        ],
        compiler_params=pltpu.CompilerParams(collective_id=cid, has_side_effects=True),
        name="sum_gradients",
    )(g.reshape(rows, cols, tile, LANES)).reshape(1024, LANES)


def place_kernel(adv_ref, hs_ref, o_ref):
    i = pl.program_id(0)

    @pl.when(i < 2)
    def _():
        for y in range(NB):
            o_ref[0, pl.ds(y, NZ, stride=NB), :] = adv_ref[0, y]

    @pl.when(i >= 2)
    def _():
        for y in range(NB):
            o_ref[0, pl.ds(y, NZ, stride=NB), :] = hs_ref[0, y]


def place(adv, hs):
    block = lambda index: pl.BlockSpec((1, NB, NZ, LANES), index)
    return pl.pallas_call(
        place_kernel,
        grid=(4,),
        in_specs=[
            block(lambda i: (jnp.minimum(i, 1), 0, 0, 0)),
            block(lambda i: (jnp.maximum(i - 2, 0), 0, 0, 0)),
        ],
        out_specs=pl.BlockSpec((1, NZ * NB, LANES), lambda i: (i + (i >= 2), 0, 0)),
        out_shape=jax.ShapeDtypeStruct((5, NZ * NB, LANES), F32),
        cost_estimate=pl.CostEstimate(flops=1_000_000, bytes_accessed=8_400_000, transcendentals=0),
        name="place",
    )(adv, hs)


def finish_kernel(rows, *refs):
    pieces = refs[:rows]
    adv_ref, depth_ref, ocean_ref, ih_ref, il_ref, _, o_ref, p_ref, buf = refs[rows:]
    r = lax.axis_index("rows")
    ids = level_ids()
    depth = depth_of(ocean_ref[...], depth_ref[...])
    for part in range(NB // 8):
        gather_levels(pieces, rows, buf, part * 8)
        hi, lo = split(buf[...])
        pressure = dot3(ih_ref[r], il_ref[r], hi, lo)
        for yi in range(8):
            y = part * 8 + yi
            p = pressure[:, yi * LANES : (yi + 1) * LANES]
            p_ref[pl.ds(y, NZ, stride=NB), :] = p
            new_w = jnp.where(ids < depth[y : y + 1, :], adv_ref[0, y] - TIME_STEP * dz(p, ids), 0.0)
            o_ref[0, pl.ds(y, NZ, stride=NB), :] = new_w


def finish(pieces, adv, depth, ocean, inv, placed, rows):
    size = NZ // rows
    full = lambda shape: pl.BlockSpec(shape, lambda i: (0,) * len(shape))
    return pl.pallas_call(
        functools.partial(finish_kernel, rows),
        grid=(1,),
        in_specs=[full((NB, size, LANES))] * rows
        + [
            pl.BlockSpec((1, NB, NZ, LANES), lambda i: (2, 0, 0, 0)),
            full((NB, LANES)), full((NB, LANES)), full((rows, NZ, NZ)), full((rows, NZ, NZ)), ANY,
        ],
        out_specs=[pl.BlockSpec((1, NZ * NB, LANES), lambda i: (2, 0, 0)), full((NZ * NB, LANES))],
        out_shape=[
            jax.ShapeDtypeStruct((5, NZ * NB, LANES), F32),
            jax.ShapeDtypeStruct((NZ * NB, LANES), F32),
        ],
        scratch_shapes=[pltpu.VMEM((NZ, 1024), F32)],
        input_output_aliases={rows + 5: 0},
        cost_estimate=pl.CostEstimate(flops=50_000_000, bytes_accessed=4_200_000, transcendentals=0),
        name="finish",
    )(*pieces, adv, depth, ocean, *inv, placed)


def shift_pieces(pieces, rows):
    got = [pieces[0]]
    for s in range(1, rows):
        got.append(lax.ppermute(pieces[s], "rows", [(i, (i + s) % rows) for i in range(rows)]))
    return got


def per_device(rows, cols, fields, cotangent, ocean, depth, in_weight, in_bias, out_weight):
    fwd, inv = level_tables(rows)
    east_np = dct_np(rows * LANES)
    east_fwd = hi_lo_np(east_np.T)
    east_inv = hi_lo_np(np.stack(np.split(east_np, rows, axis=1)))
    levels = jnp.asarray(np.repeat((SPECTRAL_SHIFT + eigen_np(NZ))[:, None], rows * LANES, 1), F32)
    easts = jnp.asarray(eigen_np(rows * LANES)[None, :], F32)
    b_in = in_bias[:, None]
    wout = jnp.pad(out_weight, ((0, 0), (0, 1)))

    ft, own, lo, hi = pack(fields, ocean, depth)
    up_r = [(i, i + 1) for i in range(rows - 1)]
    up_c = [(i, i + 1) for i in range(cols - 1)]
    down_r = [(b, a) for a, b in up_r]
    down_c = [(b, a) for a, b in up_c]
    south = lax.ppermute(hi, "cols", up_c)
    north = lax.ppermute(lo, "cols", down_c)
    west = lax.ppermute(own, "rows", up_r)
    east = lax.ppermute(own, "rows", down_r)

    adj = shift_pieces(adjoint_source(cotangent, ocean, depth, fwd, rows), rows)
    adv, spread = advect(ft, own, east, west, south, north, depth, ocean)

    v, moments = line_solve(adj, (*east_fwd, levels, easts), rows, cols)
    c = carries(moments, rows, cols, 1)
    adj = shift_pieces(line_back(v, c, (*east_inv, levels, easts), rows, cols), rows)

    *pieces, rates, act, hs = closure_forward(adv, ft, spread, depth, ocean, in_weight, b_in, wout, fwd, rows)
    pieces = shift_pieces(pieces, rows)
    grads = closure_backward(adj, adv, cotangent, rates, act, depth, ocean, wout, inv, rows)
    placed = place(adv, hs)

    v, moments = line_solve(pieces, (*east_fwd, levels, easts), rows, cols)
    c = carries(moments, rows, cols, 1)
    pieces = shift_pieces(line_back(v, c, (*east_inv, levels, easts), rows, cols), rows)
    grads = sum_gradients(grads, rows, cols, 2)
    new_fields, pressure = finish(pieces, adv, depth, ocean, inv, placed, rows)

    g_in = jnp.concatenate([grads[0:256], grads[256:512]], 1)
    g_out = jnp.concatenate([grads[512:576], grads[576:640]], 1)
    return (
        new_fields.reshape(5, NZ, NB, LANES),
        pressure.reshape(NZ, NB, LANES),
        g_in,
        g_out[NZ - 1],
        g_out[: NZ - 1].T,
    )


def solution(mesh):
    rows, cols = mesh.shape["rows"], mesh.shape["cols"]
    in_specs = (
        P(None, None, "cols", "rows"),
        P(None, None, "cols", "rows"),
        P("cols", "rows"),
        P("cols", "rows"),
        P(),
        P(),
        P(),
    )
    out_specs = (P(None, None, "cols", "rows"), P(None, "cols", "rows"), P(), P(), P())
    return jax.shard_map(
        functools.partial(per_device, rows, cols),
        mesh=mesh, in_specs=in_specs, out_specs=out_specs, check_vma=False,
    )
```

time: 820 us -> 273 us (0.33); the launches traced: 810 us -> 272 us
  waiting for transfers between devices: 354 us -> 10.3 us
  Pallas kernels: 0 us -> 224 us
  other arithmetic: 151 us -> 1.92 us
  local copies, waits for them, and re-layouts: 141 us -> 7.31 us
  matrix products: 83.7 us -> 0 us
  blocking collectives: 27.8 us -> 0 us
  between operations: 14.9 us -> 0.88 us
  starting transfers between devices: 37.3 us -> 28 us
    psum x2 -> x0, waiting for transfers between devices: 272 us -> none  [per_device(): lax.psum((grads[0], grads[1], grads[2]), ('rows', 'cols'))]
    pallas_call x0 -> x14, Pallas kernels: none -> 224 us  [the longest x1 88.5 us: advect(): pl.pallas_call(advect_kernel, grid=(NZ // 8,), in_specs=[pl.BlockSpec((5,...]
    add x15 -> x0, other arithmetic: 98.7 us -> none  [the longest x10 95.5 us: flux_tendency(): jnp.maximum(face_speed, 0.0) * left_value]
    dot_general x11 -> x0, matrix products: 83.7 us -> none  [the longest x1 28.3 us: horizontal_pencil(): gathered = jnp.einsum('ky,pyx->pkx', north_matrix, gathered, precision=high)]
    all_to_all x3 -> x0, waiting for transfers between devices: 77.1 us -> none  [the longest x2 51.2 us: column_swap(): lax.all_to_all(block, 'cols', split_axis=0, concat_axis=1, tiled=True)]
    all_to_all x3 -> x0, starting transfers between devices: 29.2 us -> none  [the longest x2 24.5 us: column_swap(): lax.all_to_all(block, 'cols', split_axis=0, concat_axis=1, tiled=True)]
    slice x12 -> x2, local copies, waits for them, and re-layouts: 29.9 us -> 1.77 us  [the longest x1 0.99 us: per_device(): g_in = jnp.concatenate([grads[0:256], grads[256:512]], 1)]
    all_to_all x1 -> x0, blocking collectives: 27.8 us -> none  [row_swap(): lax.all_to_all(block, 'rows', split_axis=1, concat_axis=2, tiled=True)]
  transfers between devices with their start and end apart: 9 -> 16, of which waited for: 7 -> 2; matrix products, arithmetic and copies ran while one was open for 4% -> 2% of each run, Pallas kernels for 0% -> 69%
where the time goes in v1:
time: 273 us; the launch traced here: 272 us
  Pallas kernels  224 us (82%)
  starting transfers between devices  28 us (10%)
  waiting for transfers between devices  10.3 us (4%)
  local copies, waits for them, and re-layouts  7.31 us (3%)
    pallas_call x1, Pallas kernels, advect(): pl.pallas_call(advect_kernel, grid=(NZ // 8,), in_specs=[pl.BlockSpec((5,...  88.5 us
    pallas_call x2, Pallas kernels, carries(): pl.pallas_call(functools.partial(carry_kernel, rows, cols), in_specs=[VM,...  40.4 us
    pallas_call x1, Pallas kernels, sum_gradients(): pl.pallas_call(functools.partial(sum_kernel, rows, cols), in_specs=[VM],...  33.7 us
    ppermute x12, starting transfers between devices, shift_pieces(): lax.ppermute(pieces[s], 'rows', [(i, (i + s) % rows) for i in range(rows)])  19.5 us
    ppermute x12, waiting for transfers between devices, shift_pieces(): lax.ppermute(pieces[s], 'rows', [(i, (i + s) % rows) for i in range(rows)])  10.3 us
    pallas_call x1, Pallas kernels, closure_backward(): pl.pallas_call(kernel, grid=(NB // 8,), in_specs=[pl.BlockSpec((8, size,...  9.99 us
    pallas_call x2, Pallas kernels, line_solve(): pl.pallas_call(functools.partial(line_kernel, rows, cols), in_specs=[VM]...  9.57 us
    pallas_call x2, Pallas kernels, line_back(): pl.pallas_call(functools.partial(back_kernel, rows, cols), in_specs=[VM]...  9.42 us
  transfers between devices with their start and end apart: 16, of which 2 were waited for; matrix products, arithmetic and copies ran while one was open for 2% of the time, Pallas kernels for 69%

profile of v1, /device:TPU:0, one launch (start us, length us, event | category | flops | bytes accessed | tf_op | source)
XLA Modules:
  0.0 272.4 jit_solution(11736261346830880269)
XLA Ops:
  0.6 3.5 %adjoint.1 = (f32[32,16,128]{2,1,0:T(8,128)}, f32[32,16,128]{2,1,0:T(8,128)}, f32[32,16,128]{2,1,0:T(8,128)}, f32[32,16,128]{2,1,0:T(8,128)}) custom-call(f32[5,2048,128]{2,1,0:T(8,128)} %bitcast.35, s32[32,128]{1,0:T(8,128)} %refs_10_.1, s32[32,128]{1,0:T(8,128)} %refs_9_.1, bf16[4,64,64]{2,1,0:T(8,128)(2,1)} %constant.27.clone.fh_ref, ...), custom_call_target="tpu_custom_call" | custom-call | flops 10000000 | bytes 2100000 | tf_op jit(solution)/shard_map/adjoint/pallas_call | solution.py:170
  4.2 2.0 collective-permute-start.10
  6.2 3.6 %collective-permute-start.11 = (f32[32,16,128]{2,1,0:T(8,128)}, f32[32,16,128]{2,1,0:T(8,128)S(1)}, u32[]{:S(2)}, u32[]{:S(2)}) collective-permute-start(f32[32,16,128]{2,1,0:T(8,128)} %get-tuple-element.57), channel_id=1, source_target_pairs={{0,64},{32,96},{64,0},{96,32},{1,65},{33,97},{65,1},{97,33},{2,66}... | collective-permute-start | bytes 786440 | tf_op jit(solution)/shard_map/ppermute | solution.py:888
  9.8 1.0 collective-permute-start.12
  10.8 8.4 %pack.1 = (f32[5,32,64,128]{3,2,1,0:T(8,128)}, f32[656,128]{1,0:T(8,128)}, f32[968,128]{1,0:T(8,128)}, f32[968,128]{1,0:T(8,128)}) custom-call(f32[5,2048,128]{2,1,0:T(8,128)} %bitcast.39, s32[32,128]{1,0:T(8,128)} %refs_10_.1, s32[32,128]{1,0:T(8,128)} %refs_9_.1), custom_call_target="tpu_custom_call" | custom-call | flops 10000000 | bytes 12000000 | tf_op jit(solution)/shard_map/pack/pallas_call | solution.py:125
  19.2 1.3 collective-permute-start.2
  20.6 1.3 collective-permute-start.3
  21.9 1.3 collective-permute-start
  23.2 4.6 %collective-permute-start.1 = (f32[656,128]{1,0:T(8,128)}, f32[656,128]{1,0:T(8,128)S(1)}, u32[]{:S(2)}, u32[]{:S(2)}) collective-permute-start(f32[656,128]{1,0:T(8,128)} %get-tuple-element.37.own_ref), channel_id=1, source_target_pairs={{0,32},{32,64},{64,96},{1,33},{33,65},{65,97},{2,34},{34,66},{66,9... | collective-permute-start | bytes 1007624 | tf_op jit(solution)/shard_map/ppermute | solution.py:909
  28.5 4.8 %line_solve.3 = (f32[512,512]{1,0:T(8,128)}, f32[256,128]{1,0:T(8,128)}) custom-call(f32[512,128]{1,0:T(8,128)} %bitcast.57, f32[512,128]{1,0:T(8,128)} %bitcast.59, f32[512,128]{1,0:T(8,128)} %bitcast.60, f32[512,128]{1,0:T(8,128)} %bitcast.61, bf16[512,512]{1,0:T(8,128)(2,1)} %constant.31.clone.refs_4_, bf16[512,512]{1,0:T(8,128)(2,1)} %constant.32.clone.refs_5_, ...), custom_call_target="tpu_custom_call" | custom-call | flops 800000000 | bytes 4500000 | tf_op jit(solution)/shard_map/line_solve/pallas_call | solution.py:476
  33.3 23.0 %carries.3 = f32[32,8,128]{2,1,0:T(8,128)} custom-call(f32[32,8,128]{2,1,0:T(8,128)} %bitcast.47, f32[64]{0:T(128)} %constant.37.clone.lv_ref, f32[2,8,128]{2,1,0:T(8,128)} %constant.38.clone.ex_ref), custom_call_target="tpu_custom_call" | custom-call | tf_op jit(solution)/shard_map/carries/pallas_call | solution.py:572
  56.3 4.7 %line_back.3 = (f32[512,128]{1,0:T(8,128)}, f32[512,128]{1,0:T(8,128)}, f32[512,128]{1,0:T(8,128)}, f32[512,128]{1,0:T(8,128)}) custom-call(f32[512,512]{1,0:T(8,128)} %get-tuple-element.59.v_ref, f32[256,128]{1,0:T(8,128)} %bitcast.46, bf16[4,512,128]{2,1,0:T(8,128)(2,1)} %constant.33.clone.ch_ref, bf16[4,512,128]{2,1,0:T(8,128)(2,1)} %constant.34.clone.cl_ref, ...), custom_call_target="tpu_custom_call" | custom-call | flops 800000000 | bytes 4500000 | tf_op jit(solution)/shard_map/line_back/pallas_call | solution.py:627
  61.0 1.0 collective-permute-start.13
  62.2 2.6 collective-permute-start.15
  64.9 0.8 copy.29.bin_ref
  66.4 0.8 copy-done
  67.4 88.5 %advect.1 = (f32[5,32,64,128]{3,2,1,0:T(8,128)}, f32[32,64,128]{2,1,0:T(8,128)}) custom-call(f32[5,32,64,128]{3,2,1,0:T(8,128)} %get-tuple-element.36.ft_ref.w_ref, f32[656,128]{1,0:T(8,128)} %get-tuple-element.37.own_ref, f32[656,128]{1,0:T(8,128)} %copy-done.2, f32[656,128]{1,0:T(8,128)} %copy-done.3, f32[968,128]{1,0:T(8,128)} %copy-done, ...), custom_call_target="tpu_custom_call" | custom-call | flops 200000000 | bytes 130000000 | tf_op jit(solution)/shard_map/advect/pallas_call | solution.py:318
  155.9 8.3 %closure_forward.1 = (f32[32,16,128]{2,1,0:T(8,128)}, f32[32,16,128]{2,1,0:T(8,128)}, f32[32,16,128]{2,1,0:T(8,128)}, f32[32,16,128]{2,1,0:T(8,128)}, f32[32,64,...) custom-call(f32[5,32,64,128]{3,2,1,0:T(8,128)} %get-tuple-element.40.adv_ref.refs_4_, ...), custom_call_target="tpu_custom_call" | custom-call | flops 900000000 | bytes 18000000 | tf_op jit(solution)/shard_map/closure_forward/pallas_call | solution.py:391
  164.6 2.4 collective-permute-start.5
  167.1 7.4 %place.1.refs_9_ = f32[5,2048,128]{2,1,0:T(8,128)} custom-call(f32[5,32,64,128]{3,2,1,0:T(8,128)} %get-tuple-element.40.adv_ref.refs_4_, f32[2,32,64,128]{3,2,1,0:T(8,128)} %get-tuple-element.52.hs_ref), custom_call_target="tpu_custom_call" | custom-call | flops 1000000 | bytes 8400000 | tf_op jit(solution)/shard_map/place/pallas_call | solution.py:830
  174.5 2.5 collective-permute-start.6
  177.8 10.0 %closure_backward.1 = f32[1024,128]{1,0:T(8,128)} custom-call(f32[32,16,128]{2,1,0:T(8,128)} %bitcast.42, f32[32,16,128]{2,1,0:T(8,128)} %copy-done.4, f32[32,16,128]{2,1,0:T(8,128)} %copy-done.5, f32[32,16,128]{2,1,0:T(8,128)} %copy-done.6, f32[5,32,64,128]{3,2,1,0:T(8,128)} %get-tuple-element.40.adv_ref.refs_4_, f32[5,64,4,8,128]{4,3,2,1,0:T(8,128)} %bitcast.36, ...), custom_call_target="tpu_custom_call" | custom-call | flops 1200000000 | bytes 16000000 | tf_op jit(solution)/shard_map/closure_backward/pallas_call | solution.py:715
  187.7 33.7 %sum_gradients.1 = f32[4,32,8,128]{3,2,1,0:T(8,128)} custom-call(f32[4,32,8,128]{3,2,1,0:T(8,128)} %bitcast.40), custom_call_target="tpu_custom_call" | custom-call | tf_op jit(solution)/shard_map/sum_gradients/pallas_call | solution.py:796
  221.4 0.8 fusion.1
  222.2 1.0 slice_bitcast_fusion.1
  224.1 4.8 %line_solve.2 = (f32[512,512]{1,0:T(8,128)}, f32[256,128]{1,0:T(8,128)}) custom-call(f32[512,128]{1,0:T(8,128)} %bitcast.54, f32[512,128]{1,0:T(8,128)} %bitcast.55, f32[512,128]{1,0:T(8,128)} %bitcast.56, f32[512,128]{1,0:T(8,128)} %bitcast.58, bf16[512,512]{1,0:T(8,128)(2,1)} %constant.31.clone.refs_4_, bf16[512,512]{1,0:T(8,128)(2,1)} %constant.32.clone.refs_5_, ...), custom_call_target="tpu_custom_call" | custom-call | flops 800000000 | bytes 4500000 | tf_op jit(solution)/shard_map/line_solve/pallas_call | solution.py:476
  228.9 17.3 %carries.2 = f32[32,8,128]{2,1,0:T(8,128)} custom-call(f32[32,8,128]{2,1,0:T(8,128)} %bitcast.45, f32[64]{0:T(128)} %constant.37.clone.lv_ref, f32[2,8,128]{2,1,0:T(8,128)} %constant.38.clone.ex_ref), custom_call_target="tpu_custom_call" | custom-call | tf_op jit(solution)/shard_map/carries/pallas_call | solution.py:572
  246.3 4.7 %line_back.2 = (f32[512,128]{1,0:T(8,128)}, f32[512,128]{1,0:T(8,128)}, f32[512,128]{1,0:T(8,128)}, f32[512,128]{1,0:T(8,128)}) custom-call(f32[512,512]{1,0:T(8,128)} %get-tuple-element.46.v_ref, f32[256,128]{1,0:T(8,128)} %bitcast.44, bf16[4,512,128]{2,1,0:T(8,128)(2,1)} %constant.33.clone.ch_ref, bf16[4,512,128]{2,1,0:T(8,128)(2,1)} %constant.34.clone.cl_ref, ...), custom_call_target="tpu_custom_call" | custom-call | flops 800000000 | bytes 4500000 | tf_op jit(solution)/shard_map/line_back/pallas_call | solution.py:627
  251.0 1.5 collective-permute-start.8
  252.5 2.2 collective-permute-start.9
  256.7 9.7 %collective-permute-done.7.refs_1_ = f32[32,16,128]{2,1,0:T(8,128)S(1)} collective-permute-done((f32[32,16,128]{2,1,0:T(8,128)}, f32[32,16,128]{2,1,0:T(8,128)S(1)}, u32[]{:S(2)}, u32[]{:S(2)}) %collective-permute-start.7) | collective-permute-done | bytes 262176 | tf_op jit(solution)/shard_map/ppermute | solution.py:888
  267.6 4.7 %finish.1 = (f32[5,2048,128]{2,1,0:T(8,128)}, f32[2048,128]{1,0:T(8,128)}) custom-call(f32[32,16,128]{2,1,0:T(8,128)} %bitcast.43, f32[32,16,128]{2,1,0:T(8,128)} %copy-done.7, f32[32,16,128]{2,1,0:T(8,128)} %copy-done.8, f32[32,16,128]{2,1,0:T(8,128)} %copy-done.9, ...), custom_call_target="tpu_custom_call", output_to_operand_aliasing={{0}: (9, {})} | custom-call | flops 50000000 | bytes 4200000 | tf_op jit(solution)/shard_map/finish/pallas_call | solution.py:865
  (60 shorter events, 7.1 us)
Async XLA Ops:
  4.2 17.7 %collective-permute-start.10 = (f32[32,16,128]{2,1,0:T(8,128)}, f32[32,16,128]{2,1,0:T(8,128)S(1)}, u32[]{:S(2)}, u32[]{:S(2)}) collective-permute-start(f32[32,16,128]{2,1,0:T(8,128)} %get-tuple-element.56), channel_id=1, source_target_pairs={{0,32},{32,64},{64,96},{96,0},{1,33},{33,65},{65,97},{97,1},{2,34}... | collective-permute-start | bytes 786440 | tf_op jit(solution)/shard_map/ppermute | solution.py:888
  6.2 17.0 %collective-permute-start.11 = (f32[32,16,128]{2,1,0:T(8,128)}, f32[32,16,128]{2,1,0:T(8,128)S(1)}, u32[]{:S(2)}, u32[]{:S(2)}) collective-permute-start(f32[32,16,128]{2,1,0:T(8,128)} %get-tuple-element.57), channel_id=1, source_target_pairs={{0,64},{32,96},{64,0},{96,32},{1,65},{33,97},{65,1},{97,33},{2,66}... | collective-permute-start | bytes 786440 | tf_op jit(solution)/shard_map/ppermute | solution.py:888
  9.8 18.0 %collective-permute-start.12 = (f32[32,16,128]{2,1,0:T(8,128)}, f32[32,16,128]{2,1,0:T(8,128)S(1)}, u32[]{:S(2)}, u32[]{:S(2)}) collective-permute-start(f32[32,16,128]{2,1,0:T(8,128)} %get-tuple-element.58), channel_id=1, source_target_pairs={{0,96},{32,0},{64,32},{96,64},{1,97},{33,1},{65,33},{97,65},{2,98}... | collective-permute-start | bytes 786440 | tf_op jit(solution)/shard_map/ppermute | solution.py:888
  10.8 54.0 %copy-start.10 = (bf16[256,63]{0,1:T(8,128)(2,1)S(1)}, bf16[256,63]{0,1:T(8,128)(2,1)}, u32[]{:S(2)}) copy-start(bf16[256,63]{0,1:T(8,128)(2,1)} %param.27) | copy-start | bytes 96772
  10.8 54.2 %copy-start.11 = (f32[256]{0:T(256)S(1)}, f32[256]{0:T(256)}, u32[]{:S(2)}) copy-start(f32[256]{0:T(256)} %param.26) | copy-start | bytes 3076
  19.2 47.1 %collective-permute-start.2 = (f32[968,128]{1,0:T(8,128)}, f32[968,128]{1,0:T(8,128)S(1)}, u32[]{:S(2)}, u32[]{:S(2)}) collective-permute-start(f32[968,128]{1,0:T(8,128)} %get-tuple-element.38), channel_id=1, source_target_pairs={{0,1},{1,2},{2,3},{3,4},{4,5},{5,6},{6,7},{7,8},{8,9},{9,10},{10,1... | collective-permute-start | bytes 1486856 | tf_op jit(solution)/shard_map/ppermute | solution.py:907
  20.6 45.8 %collective-permute-start.3 = (f32[968,128]{1,0:T(8,128)}, f32[968,128]{1,0:T(8,128)S(1)}, u32[]{:S(2)}, u32[]{:S(2)}) collective-permute-start(f32[968,128]{1,0:T(8,128)} %get-tuple-element.39), channel_id=1, source_target_pairs={{1,0},{2,1},{3,2},{4,3},{5,4},{6,5},{7,6},{8,7},{9,8},{10,9},{11,1... | collective-permute-start | bytes 1486856 | tf_op jit(solution)/shard_map/ppermute | solution.py:908
  21.9 5.9 %copy-start.16 = (f32[32,16,128]{2,1,0:T(8,128)}, f32[32,16,128]{2,1,0:T(8,128)S(1)}, u32[]{:S(2)}) copy-start(f32[32,16,128]{2,1,0:T(8,128)S(1)} %collective-permute-done.10) | copy-start | bytes 786436
  21.9 40.1 %collective-permute-start = (f32[656,128]{1,0:T(8,128)}, f32[656,128]{1,0:T(8,128)S(1)}, u32[]{:S(2)}, u32[]{:S(2)}) collective-permute-start(f32[656,128]{1,0:T(8,128)} %get-tuple-element.37.own_ref), channel_id=1, source_target_pairs={{32,0},{64,32},{96,64},{33,1},{65,33},{97,65},{34,2},{66,34},{98,6... | collective-permute-start | bytes 1007624 | tf_op jit(solution)/shard_map/ppermute | solution.py:910
  23.2 4.6 %copy-start.17 = (f32[32,16,128]{2,1,0:T(8,128)}, f32[32,16,128]{2,1,0:T(8,128)S(1)}, u32[]{:S(2)}) copy-start(f32[32,16,128]{2,1,0:T(8,128)S(1)} %collective-permute-done.11) | copy-start | bytes 786436
  23.2 39.0 %collective-permute-start.1 = (f32[656,128]{1,0:T(8,128)}, f32[656,128]{1,0:T(8,128)S(1)}, u32[]{:S(2)}, u32[]{:S(2)}) collective-permute-start(f32[656,128]{1,0:T(8,128)} %get-tuple-element.37.own_ref), channel_id=1, source_target_pairs={{0,32},{32,64},{64,96},{1,33},{33,65},{65,97},{2,34},{34,66},{66,9... | collective-permute-start | bytes 1007624 | tf_op jit(solution)/shard_map/ppermute | solution.py:909
  27.8 0.7 copy-start.18
  61.0 113.4 %collective-permute-start.13 = (f32[32,16,128]{2,1,0:T(8,128)}, f32[32,16,128]{2,1,0:T(8,128)S(1)}, u32[]{:S(2)}, u32[]{:S(2)}) collective-permute-start(f32[32,16,128]{2,1,0:T(8,128)} %bitcast.53), channel_id=1, source_target_pairs={{0,32},{32,64},{64,96},{96,0},{1,33},{33,65},{65,97},{97,1},{2,34}... | collective-permute-start | bytes 786440 | tf_op jit(solution)/shard_map/ppermute | solution.py:888
  62.0 4.4 %copy-start.2 = (f32[656,128]{1,0:T(8,128)}, f32[656,128]{1,0:T(8,128)S(1)}, u32[]{:S(2)}) copy-start(f32[656,128]{1,0:T(8,128)S(1)} %collective-permute-done.east_ref) | copy-start | bytes 1007620
  62.0 114.9 %collective-permute-start.14 = (f32[32,16,128]{2,1,0:T(8,128)}, f32[32,16,128]{2,1,0:T(8,128)S(1)}, u32[]{:S(2)}, u32[]{:S(2)}) collective-permute-start(f32[32,16,128]{2,1,0:T(8,128)} %bitcast.52), channel_id=1, source_target_pairs={{0,64},{32,96},{64,0},{96,32},{1,65},{33,97},{65,1},{97,33},{2,66}... | collective-permute-start | bytes 786440 | tf_op jit(solution)/shard_map/ppermute | solution.py:888
  62.2 4.2 %copy-start.3 = (f32[656,128]{1,0:T(8,128)}, f32[656,128]{1,0:T(8,128)S(1)}, u32[]{:S(2)}) copy-start(f32[656,128]{1,0:T(8,128)S(1)} %collective-permute-done.1.west_ref) | copy-start | bytes 1007620
  62.2 114.8 %collective-permute-start.15 = (f32[32,16,128]{2,1,0:T(8,128)}, f32[32,16,128]{2,1,0:T(8,128)S(1)}, u32[]{:S(2)}, u32[]{:S(2)}) collective-permute-start(f32[32,16,128]{2,1,0:T(8,128)} %bitcast.51), channel_id=1, source_target_pairs={{0,96},{32,0},{64,32},{96,64},{1,97},{33,1},{65,33},{97,65},{2,98}... | collective-permute-start | bytes 786440 | tf_op jit(solution)/shard_map/ppermute | solution.py:888
  66.4 0.8 copy-start
  66.4 1.0 copy-start.1
  164.2 59.0 %collective-permute-start.4 = (f32[32,16,128]{2,1,0:T(8,128)}, f32[32,16,128]{2,1,0:T(8,128)S(1)}, u32[]{:S(2)}, u32[]{:S(2)}) collective-permute-start(f32[32,16,128]{2,1,0:T(8,128)} %get-tuple-element.43), channel_id=1, source_target_pairs={{0,32},{32,64},{64,96},{96,0},{1,33},{33,65},{65,97},{97,1},{2,34}... | collective-permute-start | bytes 786440 | tf_op jit(solution)/shard_map/ppermute | solution.py:888
  164.6 58.6 %collective-permute-start.5 = (f32[32,16,128]{2,1,0:T(8,128)}, f32[32,16,128]{2,1,0:T(8,128)S(1)}, u32[]{:S(2)}, u32[]{:S(2)}) collective-permute-start(f32[32,16,128]{2,1,0:T(8,128)} %get-tuple-element.44), channel_id=1, source_target_pairs={{0,64},{32,96},{64,0},{96,32},{1,65},{33,97},{65,1},{97,33},{2,66}... | collective-permute-start | bytes 786440 | tf_op jit(solution)/shard_map/ppermute | solution.py:888
  167.0 7.4 %copy-start.12 = (f32[32,16,128]{2,1,0:T(8,128)S(1)}, f32[32,16,128]{2,1,0:T(8,128)}, u32[]{:S(2)}) copy-start(f32[32,16,128]{2,1,0:T(8,128)} %get-tuple-element.45) | copy-start | bytes 786436
  174.4 2.5 copy-start.4
  174.5 48.8 %collective-permute-start.6 = (f32[32,16,128]{2,1,0:T(8,128)S(1)}, f32[32,16,128]{2,1,0:T(8,128)S(1)}, u32[]{:S(2)}, u32[]{:S(2)}) collective-permute-start(f32[32,16,128]{2,1,0:T(8,128)S(1)} %copy-done.12), channel_id=1, source_target_pairs={{0,96},{32,0},{64,32},{96,64},{1,97},{33,1},{65,33},{97,65},{2,98}... | collective-permute-start | bytes 786440 | tf_op jit(solution)/shard_map/ppermute | solution.py:888
  177.0 0.8 copy-start.6
  223.2 0.7 copy-start.13
  223.2 0.8 copy-start.14
  223.3 0.9 copy-start.15
  251.0 15.4 %collective-permute-start.7 = (f32[32,16,128]{2,1,0:T(8,128)}, f32[32,16,128]{2,1,0:T(8,128)S(1)}, u32[]{:S(2)}, u32[]{:S(2)}) collective-permute-start(f32[32,16,128]{2,1,0:T(8,128)} %bitcast.64), channel_id=1, source_target_pairs={{0,32},{32,64},{64,96},{96,0},{1,33},{33,65},{65,97},{97,1},{2,34}... | collective-permute-start | bytes 786440 | tf_op jit(solution)/shard_map/ppermute | solution.py:888
  251.0 15.4 %collective-permute-start.8 = (f32[32,16,128]{2,1,0:T(8,128)}, f32[32,16,128]{2,1,0:T(8,128)S(1)}, u32[]{:S(2)}, u32[]{:S(2)}) collective-permute-start(f32[32,16,128]{2,1,0:T(8,128)} %bitcast.63), channel_id=1, source_target_pairs={{0,64},{32,96},{64,0},{96,32},{1,65},{33,97},{65,1},{97,33},{2,66}... | collective-permute-start | bytes 786440 | tf_op jit(solution)/shard_map/ppermute | solution.py:888
  252.5 14.4 %collective-permute-start.9 = (f32[32,16,128]{2,1,0:T(8,128)}, f32[32,16,128]{2,1,0:T(8,128)S(1)}, u32[]{:S(2)}, u32[]{:S(2)}) collective-permute-start(f32[32,16,128]{2,1,0:T(8,128)} %bitcast.62), channel_id=1, source_target_pairs={{0,96},{32,0},{64,32},{96,64},{1,97},{33,1},{65,33},{97,65},{2,98}... | collective-permute-start | bytes 786440 | tf_op jit(solution)/shard_map/ppermute | solution.py:888
  266.3 0.8 copy-start.8
  (3 other events, 2.1 us)

commit v2 on v1

--- a/solution.py
+++ b/solution.py
@@ -217,7 +217,7 @@
 
 
 def advect_kernel(ft_ref, own_ref, east_ref, west_ref, south_ref, north_ref, depth_ref, ocean_ref,
-                  adv_ref, spread_ref, ext, dext, exy, fxe, edge_d):
+                  adv_ref, spread_ref, ext, dd, dfx, dfy, dfp, exy, fxe):
     zb = pl.program_id(0)
     z0 = pl.multiple_of(zb * 8, 8)
     zf = (lax.broadcasted_iota(jnp.int32, (8, LANES), 0) + z0).astype(F32)
@@ -226,10 +226,26 @@
     first, second = lane == 0, lane <= 1
     last, last2 = lane == LANES - 1, lane >= LANES - 2
 
-    depth = depth_of(ocean_ref[...], depth_ref[...]).astype(F32)
-    dext[8:40] = depth
-    dext[7:8] = south_ref[960:961]
-    dext[40:41] = north_ref[960:961]
+    @pl.when(zb == 0)
+    def _():
+        depth = depth_of(ocean_ref[...], depth_ref[...]).astype(F32)
+        before = south_ref[960:968]
+        for y in range(NB):
+            g, yi = y // 16, y % 16
+            d8 = jnp.broadcast_to(depth[y : y + 1], (8, LANES))
+            at_d = pl.ds(640 + g * 8, 8)
+            ed = jnp.where(in_hi, east_ref[at_d], west_ref[at_d])
+            ed = pltpu.roll(ed, LANES - 8 * yi, 1) if yi else ed
+            dd[y] = d8
+            dfy[y] = jnp.minimum(before, d8)
+            dfx[y] = jnp.minimum(d8, pltpu.roll(jnp.where(last, ed, d8), 1, 1))
+            before = d8
+        dfy[NB] = jnp.minimum(before, north_ref[960:968])
+        for g in range(2):
+            at_d = pl.ds(640 + g * 8, 8)
+            d_face = jnp.where(in_hi, east_ref[at_d], own_ref[at_d])
+            dfp[g] = jnp.minimum(d_face, pltpu.roll(d_face, 1, 1))
+
     for f in range(5):
         for r in range(3):
             at = pl.ds(pl.multiple_of((f * 3 + r) * NZ + z0, 8), 8)
@@ -238,10 +254,7 @@
         ext[f, 3 : 3 + NB] = ft_ref[f]
 
     for g in range(2):
-        at_d = pl.ds(640 + g * 8, 8)
-        edge_d[g] = jnp.where(in_hi, east_ref[at_d], west_ref[at_d])
-        d_face = jnp.where(in_hi, east_ref[at_d], own_ref[at_d])
-        d_face = jnp.minimum(d_face, pltpu.roll(d_face, 1, 1))
+        d_face = dfp[g]
         for f in range(5):
             at = pl.ds(pl.multiple_of((f * 2 + g) * NZ + z0, 8), 8)
             exy[f, g] = jnp.where(in_hi, east_ref[at], west_ref[at])
@@ -258,7 +271,7 @@
             )
 
     def face_y(j):
-        d_face = jnp.minimum(dext[pl.ds(j + 7, 1), :], dext[pl.ds(j + 8, 1), :])
+        d_face = dfy[j]
         out = []
         v = [ext[1, j + 2], ext[1, j + 3]]
         speed = jnp.where(zf < d_face, 0.5 * (v[0] + v[1]), 0.0)
@@ -280,11 +293,8 @@
         yi = lax.rem(j, 16)
         back = lax.rem(LANES - 8 * yi, LANES)
         to_last = LANES - 1 - 8 * yi
-        drow = dext[pl.ds(j + 8, 1), :]
-        d8 = jnp.broadcast_to(drow, (8, LANES))
-        ed = pltpu.roll(edge_d[g], back, 1)
-        d_face = jnp.minimum(d8, pltpu.roll(jnp.where(last, ed, d8), 1, 1))
-        wet = zf < d8
+        d_face = dfx[j]
+        wet = zf < dd[j]
         du = None
         for f in range(5):
             q = ext[f, j + 3]
@@ -310,7 +320,7 @@
         spread_ref[j] = 0.5 * du + 0.5 * (below_dv + above_dv)
         return above_flux, above_dv
 
-    lax.fori_loop(0, NB, step, face_y(0))
+    lax.fori_loop(0, NB, step, face_y(0), unroll=4)
 
 
 def advect(ft, own, east, west, south, north, depth, ocean):
@@ -334,10 +344,12 @@
         ],
         scratch_shapes=[
             pltpu.VMEM((5, NB + 6, 8, LANES), F32),
-            pltpu.VMEM((48, LANES), F32),
+            pltpu.VMEM((NB, 8, LANES), F32),
+            pltpu.VMEM((NB, 8, LANES), F32),
+            pltpu.VMEM((NB + 1, 8, LANES), F32),
+            pltpu.VMEM((2, 8, LANES), F32),
             pltpu.VMEM((5, 2, 8, LANES), F32),
             pltpu.VMEM((5, 2, 8, LANES), F32),
-            pltpu.VMEM((2, 8, LANES), F32),
         ],
         cost_estimate=pl.CostEstimate(flops=200_000_000, bytes_accessed=130_000_000, transcendentals=0),
         name="advect",
@@ -487,7 +499,7 @@
     )(*[p.reshape(NB * size, LANES) for p in pieces], *tables)
 
 
-def carry_kernel(rows, cols, s_ref, lv_ref, ex_ref, c_ref, got, send, dsem, send_sem, recv_sem, send2_sem, recv2_sem):
+def carry_kernel(rows, cols, s_ref, lv_ref, ex_ref, c_ref, got, send, up, down, dsem, send_sem, recv_sem):
     n = NZ // cols
     tile = max(8, 2 * n)
     me = lax.axis_index("cols")
@@ -504,22 +516,24 @@
     def out_copy(t):
         peer = lax.rem(me + t, cols)
         return pltpu.make_async_remote_copy(
-            src_ref=s_ref.at[peer], dst_ref=got.at[me], send_sem=send_sem.at[t], recv_sem=recv_sem.at[t],
+            src_ref=s_ref.at[peer], dst_ref=got.at[me], send_sem=send_sem.at[0], recv_sem=recv_sem.at[0],
             device_id={"cols": peer}, device_id_type=MESH,
         )
 
     def back_copy(t):
         peer = lax.rem(me + t, cols)
         return pltpu.make_async_remote_copy(
-            src_ref=send.at[peer], dst_ref=c_ref.at[me], send_sem=send2_sem.at[t], recv_sem=recv2_sem.at[t],
+            src_ref=send.at[peer], dst_ref=c_ref.at[me], send_sem=send_sem.at[1], recv_sem=recv_sem.at[1],
             device_id={"cols": peer}, device_id_type=MESH,
         )
 
     def run(make):
         lax.fori_loop(1, cols, lambda t, c: (make(t).start(), c)[1], 0)
 
-    def finish(make):
-        lax.fori_loop(1, cols, lambda t, c: (make(t).wait(), c)[1], 0)
+    def finish(i):
+        others = got.at[pl.ds(0, cols - 1)]
+        pltpu.make_async_copy(others, others, recv_sem.at[i]).wait()
+        pltpu.make_async_copy(others, others, send_sem.at[i]).wait()
 
     run(out_copy)
     mine = pltpu.make_async_copy(s_ref.at[me], got.at[me], dsem.at[0])
@@ -537,31 +551,28 @@
     scale = 1.0 / (1.0 - whole * whole)
     is_start = lax.broadcasted_iota(jnp.int32, (tile, LANES), 0) < n
     mine.wait()
-    finish(out_copy)
+    finish(0)
 
     zero = jnp.zeros((tile, LANES), F32)
-    sa = lax.fori_loop(0, cols, lambda k, a: got[cols - 1 - k] + mu * a, zero)
-    sb = lax.fori_loop(0, cols, lambda k, b: got[k] + mu * b, zero)
+    sa, sb = lax.fori_loop(
+        0, cols, lambda k, c: (got[cols - 1 - k] + mu * c[0], got[k] + mu * c[1]), (zero, zero), unroll=8
+    )
     left = (pltpu.roll(sa, n, 0) + whole * sb) * scale
     right = (pltpu.roll(sb, tile - n, 0) + whole * sa) * scale
 
-    def ascend(k, c):
-        send[k] = c
-        return got[k] + mu * c
-
-    lax.fori_loop(0, cols, ascend, left)
-
-    def descend(i, c):
-        k = cols - 1 - i
-        send[k] = jnp.where(is_start, c, send[k])
-        return got[k] + mu * c
-
-    lax.fori_loop(0, cols, descend, right)
+    def both(k, c):
+        m = cols - 1 - k
+        up[k] = c[0]
+        down[m] = c[1]
+        return got[k] + mu * c[0], got[m] + mu * c[1]
+
+    lax.fori_loop(0, cols, both, (left, right), unroll=8)
+    send[...] = jnp.where(is_start, down[...], up[...])
     run(back_copy)
     mine2 = pltpu.make_async_copy(send.at[me], c_ref.at[me], dsem.at[1])
     mine2.start()
     mine2.wait()
-    finish(back_copy)
+    finish(1)
 
 
 def carries(moments, rows, cols, cid):
@@ -577,11 +588,11 @@
         scratch_shapes=[
             pltpu.VMEM((cols, tile, LANES), F32),
             pltpu.VMEM((cols, tile, LANES), F32),
+            pltpu.VMEM((cols, tile, LANES), F32),
+            pltpu.VMEM((cols, tile, LANES), F32),
             pltpu.SemaphoreType.DMA((2,)),
-            pltpu.SemaphoreType.DMA((cols,)),
-            pltpu.SemaphoreType.DMA((cols,)),
-            pltpu.SemaphoreType.DMA((cols,)),
-            pltpu.SemaphoreType.DMA((cols,)),
+            pltpu.SemaphoreType.DMA((2,)),
+            pltpu.SemaphoreType.DMA((2,)),
         ],
         compiler_params=pltpu.CompilerParams(collective_id=cid, has_side_effects=True),
         name="carries",
@@ -737,7 +748,7 @@
     )(*pieces, adv, cot, cot, rates, act, depth, ocean, wout, *inv)
 
 
-def sum_kernel(rows, cols, g_ref, o_ref, land, acc, land2, total, dsem, s1, r1, s2, r2, s3, r3, s4, r4):
+def sum_kernel(rows, cols, g_ref, o_ref, land, acc, land2, total, tile_ref, dsem, send_sem, recv_sem):
     me = lax.axis_index("cols")
     r = lax.axis_index("rows")
     barrier = pltpu.get_barrier_semaphore()
@@ -751,48 +762,48 @@
         pl.semaphore_signal(barrier, inc=1, device_id={"rows": lax.rem(r + t, rows)}, device_id_type=MESH)
     pl.semaphore_wait(barrier, cols - 1 + rows - 1)
 
-    def copy(axis, count, at, t, src, dst, ss, rs):
+    def copy(axis, count, at, t, src, dst, i):
         return pltpu.make_async_remote_copy(
-            src_ref=src, dst_ref=dst, send_sem=ss.at[t], recv_sem=rs.at[t],
+            src_ref=src, dst_ref=dst, send_sem=send_sem.at[i], recv_sem=recv_sem.at[i],
             device_id={axis: lax.rem(at + t, count)}, device_id_type=MESH,
         )
 
     def rows_out(t):
-        return copy("rows", rows, r, t, g_ref.at[lax.rem(r + t, rows)], land.at[t], s1, r1)
+        return copy("rows", rows, r, t, g_ref.at[lax.rem(r + t, rows)], land.at[t], 0)
 
     def cols_out(t):
-        return copy("cols", cols, me, t, acc.at[lax.rem(me + t, cols)], land2.at[t], s2, r2)
+        return copy("cols", cols, me, t, acc.at[lax.rem(me + t, cols)], land2.at[t], 1)
 
     def cols_back(t):
-        return copy("cols", cols, me, t, total.at[me], total.at[me], s3, r3)
+        return copy("cols", cols, me, t, tile_ref, total.at[me], 2)
 
     def rows_back(t):
-        return copy("rows", rows, r, t, total, o_ref.at[r], s4, r4)
-
-    def all_of(make, count):
+        return copy("rows", rows, r, t, total, o_ref.at[r], 3)
+
+    def all_of(make, count, ref, i):
         lax.fori_loop(1, count, lambda t, c: (make(t).start(), c)[1], 0)
-        lax.fori_loop(1, count, lambda t, c: (make(t).wait(), c)[1], 0)
-
-    all_of(rows_out, rows)
+        others = ref.at[pl.ds(0, count - 1)]
+        pltpu.make_async_copy(others, others, recv_sem.at[i]).wait()
+        pltpu.make_async_copy(others, others, send_sem.at[i]).wait()
+
+    all_of(rows_out, rows, land, 0)
     value = g_ref[r]
     for t in range(1, rows):
         value = value + land[t]
     acc[...] = value
-    all_of(cols_out, cols)
-    tile = lax.fori_loop(1, cols, lambda t, v: v + land2[t], acc[me])
-    total[me] = tile
-    all_of(cols_back, cols)
+    all_of(cols_out, cols, land2, 1)
+    value = lax.fori_loop(1, cols, lambda t, v: v + land2[t], acc[me])
+    tile_ref[...] = value
+    total[me] = value
+    all_of(cols_back, cols, land2, 2)
     own = pltpu.make_async_copy(total, o_ref.at[r], dsem.at[0])
     own.start()
-    all_of(rows_back, rows)
+    all_of(rows_back, rows, land, 3)
     own.wait()
 
 
 def sum_gradients(g, rows, cols, cid):
     tile = 1024 // (rows * cols)
-    sems = []
-    for count in (rows, cols, cols, rows):
-        sems += [pltpu.SemaphoreType.DMA((count,)), pltpu.SemaphoreType.DMA((count,))]
     return pl.pallas_call(
         functools.partial(sum_kernel, rows, cols),
         in_specs=[VM],
@@ -803,8 +814,10 @@
             pltpu.VMEM((cols, tile, LANES), F32),
             pltpu.VMEM((cols, tile, LANES), F32),
             pltpu.VMEM((cols, tile, LANES), F32),
+            pltpu.VMEM((tile, LANES), F32),
             pltpu.SemaphoreType.DMA((1,)),
-            *sems,
+            pltpu.SemaphoreType.DMA((4,)),
+            pltpu.SemaphoreType.DMA((4,)),
         ],
         compiler_params=pltpu.CompilerParams(collective_id=cid, has_side_effects=True),
         name="sum_gradients",
@@ -923,7 +936,9 @@
 
     v, moments = line_solve(pieces, (*east_fwd, levels, easts), rows, cols)
     c = carries(moments, rows, cols, 1)
-    pieces = shift_pieces(line_back(v, c, (*east_inv, levels, easts), rows, cols), rows)
+    pieces = line_back(v, c, (*east_inv, levels, easts), rows, cols)
+    grads, pieces[0] = lax.optimization_barrier((grads, pieces[0]))
+    pieces = shift_pieces(pieces, rows)
     grads = sum_gradients(grads, rows, cols, 2)
     new_fields, pressure = finish(pieces, adv, depth, ocean, inv, placed, rows)
 

time: 273 us -> 218 us (0.80)
  Pallas kernels: 224 us -> 169 us
    pallas_call x1, Pallas kernels: 88.5 us -> 38.9 us  [advect(): pl.pallas_call(advect_kernel, grid=(NZ // 8,), in_specs=[pl.BlockSpec((5,...]
    pallas_call x2, Pallas kernels: 40.4 us -> 36.6 us  [carries(): pl.pallas_call(functools.partial(carry_kernel, rows, cols), in_specs=[VM,...]
  transfers between devices with their start and end apart: 16 -> 16, of which waited for: 2 -> 2; matrix products, arithmetic and copies ran while one was open for 2% -> 2% of each run, Pallas kernels for 69% -> 48%
where the time goes in v2:
time: 218 us; the launch traced here: 217 us
  Pallas kernels  169 us (78%)
  starting transfers between devices  27.7 us (13%)
  waiting for transfers between devices  9.71 us (4%)
  local copies, waits for them, and re-layouts  7.49 us (3%)
    pallas_call x1, Pallas kernels, advect(): pl.pallas_call(advect_kernel, grid=(NZ // 8,), in_specs=[pl.BlockSpec((5,...  38.9 us
    pallas_call x2, Pallas kernels, carries(): pl.pallas_call(functools.partial(carry_kernel, rows, cols), in_specs=[VM,...  36.6 us
    pallas_call x1, Pallas kernels, sum_gradients(): pl.pallas_call(functools.partial(sum_kernel, rows, cols), in_specs=[VM],...  32.3 us
    ppermute x12, starting transfers between devices, shift_pieces(): lax.ppermute(pieces[s], 'rows', [(i, (i + s) % rows) for i in range(rows)])  19.3 us
    pallas_call x1, Pallas kernels, closure_backward(): pl.pallas_call(kernel, grid=(NB // 8,), in_specs=[pl.BlockSpec((8, size,...  10 us
    ppermute x12, waiting for transfers between devices, shift_pieces(): lax.ppermute(pieces[s], 'rows', [(i, (i + s) % rows) for i in range(rows)])  9.7 us
    pallas_call x2, Pallas kernels, line_solve(): pl.pallas_call(functools.partial(line_kernel, rows, cols), in_specs=[VM]...  9.59 us
    pallas_call x2, Pallas kernels, line_back(): pl.pallas_call(functools.partial(back_kernel, rows, cols), in_specs=[VM]...  9.44 us
  transfers between devices with their start and end apart: 16, of which 2 were waited for; matrix products, arithmetic and copies ran while one was open for 2% of the time, Pallas kernels for 48%

profile of v2, /device:TPU:0, one launch (start us, length us, event | category | flops | bytes accessed | tf_op | source)
XLA Modules:
  0.0 216.9 jit_solution(9402062050048070134)
XLA Ops:
  0.6 3.5 %adjoint.1 = (f32[32,16,128]{2,1,0:T(8,128)}, f32[32,16,128]{2,1,0:T(8,128)}, f32[32,16,128]{2,1,0:T(8,128)}, f32[32,16,128]{2,1,0:T(8,128)}) custom-call(f32[5,2048,128]{2,1,0:T(8,128)} %bitcast.35, s32[32,128]{1,0:T(8,128)} %refs_6_.3, s32[32,128]{1,0:T(8,128)} %refs_5_.3, bf16[4,64,64]{2,1,0:T(8,128)(2,1)} %constant.27.clone.fh_ref, ...), custom_call_target="tpu_custom_call" | custom-call | flops 10000000 | bytes 2100000 | tf_op jit(solution)/shard_map/adjoint/pallas_call | solution.py:170
  4.2 2.0 collective-permute-start
  6.2 3.6 %collective-permute-start.1 = (f32[32,16,128]{2,1,0:T(8,128)}, f32[32,16,128]{2,1,0:T(8,128)S(1)}, u32[]{:S(2)}, u32[]{:S(2)}) collective-permute-start(f32[32,16,128]{2,1,0:T(8,128)} %get-tuple-element.40), channel_id=1, source_target_pairs={{0,64},{32,96},{64,0},{96,32},{1,65},{33,97},{65,1},{97,33},{2,66}... | collective-permute-start | bytes 786440 | tf_op jit(solution)/shard_map/ppermute | solution.py:901
  9.8 1.0 collective-permute-start.2
  10.8 8.4 %pack.1 = (f32[5,32,64,128]{3,2,1,0:T(8,128)}, f32[656,128]{1,0:T(8,128)}, f32[968,128]{1,0:T(8,128)}, f32[968,128]{1,0:T(8,128)}) custom-call(f32[5,2048,128]{2,1,0:T(8,128)} %bitcast.39, s32[32,128]{1,0:T(8,128)} %refs_6_.3, s32[32,128]{1,0:T(8,128)} %refs_5_.3), custom_call_target="tpu_custom_call" | custom-call | flops 10000000 | bytes 12000000 | tf_op jit(solution)/shard_map/pack/pallas_call | solution.py:125
  19.2 1.3 collective-permute-start.8
  20.6 1.3 collective-permute-start.9
  21.9 1.3 collective-permute-start.6
  23.2 4.6 %collective-permute-start.7 = (f32[656,128]{1,0:T(8,128)}, f32[656,128]{1,0:T(8,128)S(1)}, u32[]{:S(2)}, u32[]{:S(2)}) collective-permute-start(f32[656,128]{1,0:T(8,128)} %get-tuple-element.49.own_ref), channel_id=1, source_target_pairs={{0,32},{32,64},{64,96},{1,33},{33,65},{65,97},{2,34},{34,66},{66,9... | collective-permute-start | bytes 1007624 | tf_op jit(solution)/shard_map/ppermute | solution.py:922
  28.5 4.8 %line_solve.2 = (f32[512,512]{1,0:T(8,128)}, f32[256,128]{1,0:T(8,128)}) custom-call(f32[512,128]{1,0:T(8,128)} %bitcast.56, f32[512,128]{1,0:T(8,128)} %bitcast.58, f32[512,128]{1,0:T(8,128)} %bitcast.60, f32[512,128]{1,0:T(8,128)} %bitcast.62, bf16[512,512]{1,0:T(8,128)(2,1)} %constant.31.clone.refs_4_, bf16[512,512]{1,0:T(8,128)(2,1)} %constant.32.clone.refs_5_, ...), custom_call_target="tpu_custom_call" | custom-call | flops 800000000 | bytes 4500000 | tf_op jit(solution)/shard_map/line_solve/pallas_call | solution.py:488
  33.3 21.2 %carries.2 = f32[32,8,128]{2,1,0:T(8,128)} custom-call(f32[32,8,128]{2,1,0:T(8,128)} %bitcast.47, f32[64]{0:T(128)} %constant.37.clone.lv_ref, f32[2,8,128]{2,1,0:T(8,128)} %constant.38.clone.ex_ref), custom_call_target="tpu_custom_call" | custom-call | tf_op jit(solution)/shard_map/carries/pallas_call | solution.py:583
  54.4 4.7 %line_back.2 = (f32[512,128]{1,0:T(8,128)}, f32[512,128]{1,0:T(8,128)}, f32[512,128]{1,0:T(8,128)}, f32[512,128]{1,0:T(8,128)}) custom-call(f32[512,512]{1,0:T(8,128)} %get-tuple-element.42.v_ref, f32[256,128]{1,0:T(8,128)} %bitcast.46, bf16[4,512,128]{2,1,0:T(8,128)(2,1)} %constant.33.clone.ch_ref, bf16[4,512,128]{2,1,0:T(8,128)(2,1)} %constant.34.clone.cl_ref, ...), custom_call_target="tpu_custom_call" | custom-call | flops 800000000 | bytes 4500000 | tf_op jit(solution)/shard_map/line_back/pallas_call | solution.py:638
  59.1 1.0 collective-permute-start.3
  60.3 2.6 %collective-permute-start.5 = (f32[32,16,128]{2,1,0:T(8,128)}, f32[32,16,128]{2,1,0:T(8,128)S(1)}, u32[]{:S(2)}, u32[]{:S(2)}) collective-permute-start(f32[32,16,128]{2,1,0:T(8,128)} %bitcast.51), channel_id=1, source_target_pairs={{0,96},{32,0},{64,32},{96,64},{1,97},{33,1},{65,33},{97,65},{2,98}... | collective-permute-start | bytes 786440 | tf_op jit(solution)/shard_map/ppermute | solution.py:901
  63.1 0.8 copy.29.bin_ref
  64.5 0.7 copy-done
  65.5 38.9 %advect.1 = (f32[5,32,64,128]{3,2,1,0:T(8,128)}, f32[32,64,128]{2,1,0:T(8,128)}) custom-call(f32[5,32,64,128]{3,2,1,0:T(8,128)} %get-tuple-element.48.ft_ref.w_ref, f32[656,128]{1,0:T(8,128)} %get-tuple-element.49.own_ref, f32[656,128]{1,0:T(8,128)} %copy-done.2, f32[656,128]{1,0:T(8,128)} %copy-done.3, f32[968,128]{1,0:T(8,128)} %copy-done, ...), custom_call_target="tpu_custom_call" | custom-call | flops 200000000 | bytes 130000000 | tf_op jit(solution)/shard_map/advect/pallas_call | solution.py:328
  104.4 8.3 %closure_forward.1 = (f32[32,16,128]{2,1,0:T(8,128)}, f32[32,16,128]{2,1,0:T(8,128)}, f32[32,16,128]{2,1,0:T(8,128)}, f32[32,16,128]{2,1,0:T(8,128)}, f32[32,64,...) custom-call(f32[5,32,64,128]{3,2,1,0:T(8,128)} %get-tuple-element.52.adv_ref.refs_4_, ...), custom_call_target="tpu_custom_call" | custom-call | flops 900000000 | bytes 18000000 | tf_op jit(solution)/shard_map/closure_forward/pallas_call | solution.py:403
  113.1 2.5 %collective-permute-start.11 = (f32[32,16,128]{2,1,0:T(8,128)}, f32[32,16,128]{2,1,0:T(8,128)S(1)}, u32[]{:S(2)}, u32[]{:S(2)}) collective-permute-start(f32[32,16,128]{2,1,0:T(8,128)} %get-tuple-element.58), channel_id=1, source_target_pairs={{0,64},{32,96},{64,0},{96,32},{1,65},{33,97},{65,1},{97,33},{2,66}... | collective-permute-start | bytes 786440 | tf_op jit(solution)/shard_map/ppermute | solution.py:901
  115.5 2.2 %collective-permute-start.12 = (f32[32,16,128]{2,1,0:T(8,128)}, f32[32,16,128]{2,1,0:T(8,128)S(1)}, u32[]{:S(2)}, u32[]{:S(2)}) collective-permute-start(f32[32,16,128]{2,1,0:T(8,128)} %get-tuple-element.59), channel_id=1, source_target_pairs={{0,96},{32,0},{64,32},{96,64},{1,97},{33,1},{65,33},{97,65},{2,98}... | collective-permute-start | bytes 786440 | tf_op jit(solution)/shard_map/ppermute | solution.py:901
  117.8 7.3 %place.1.refs_9_ = f32[5,2048,128]{2,1,0:T(8,128)} custom-call(f32[5,32,64,128]{3,2,1,0:T(8,128)} %get-tuple-element.52.adv_ref.refs_4_, f32[2,32,64,128]{3,2,1,0:T(8,128)} %get-tuple-element.67.hs_ref), custom_call_target="tpu_custom_call" | custom-call | flops 1000000 | bytes 8400000 | tf_op jit(solution)/shard_map/place/pallas_call | solution.py:843
  125.9 10.0 %closure_backward.1 = f32[1024,128]{1,0:T(8,128)} custom-call(f32[32,16,128]{2,1,0:T(8,128)} %bitcast.42, f32[32,16,128]{2,1,0:T(8,128)} %copy-done.4, f32[32,16,128]{2,1,0:T(8,128)} %copy-done.5, f32[32,16,128]{2,1,0:T(8,128)} %copy-done.6, f32[5,32,64,128]{3,2,1,0:T(8,128)} %get-tuple-element.52.adv_ref.refs_4_, f32[5,64,4,8,128]{4,3,2,1,0:T(8,128)} %bitcast.36, ...), custom_call_target="tpu_custom_call" | custom-call | flops 1200000000 | bytes 16000000 | tf_op jit(solution)/shard_map/closure_backward/pallas_call | solution.py:726
  136.8 4.8 %line_solve.3 = (f32[512,512]{1,0:T(8,128)}, f32[256,128]{1,0:T(8,128)}) custom-call(f32[512,128]{1,0:T(8,128)} %bitcast.54, f32[512,128]{1,0:T(8,128)} %bitcast.55, f32[512,128]{1,0:T(8,128)} %bitcast.57, f32[512,128]{1,0:T(8,128)} %bitcast.63, bf16[512,512]{1,0:T(8,128)(2,1)} %constant.31.clone.refs_4_, bf16[512,512]{1,0:T(8,128)(2,1)} %constant.32.clone.refs_5_, ...), custom_call_target="tpu_custom_call" | custom-call | flops 800000000 | bytes 4500000 | tf_op jit(solution)/shard_map/line_solve/pallas_call | solution.py:488
  141.6 15.4 %carries.3 = f32[32,8,128]{2,1,0:T(8,128)} custom-call(f32[32,8,128]{2,1,0:T(8,128)} %bitcast.45, f32[64]{0:T(128)} %constant.37.clone.lv_ref, f32[2,8,128]{2,1,0:T(8,128)} %constant.38.clone.ex_ref), custom_call_target="tpu_custom_call" | custom-call | tf_op jit(solution)/shard_map/carries/pallas_call | solution.py:583
  157.1 4.7 %line_back.3 = (f32[512,128]{1,0:T(8,128)}, f32[512,128]{1,0:T(8,128)}, f32[512,128]{1,0:T(8,128)}, f32[512,128]{1,0:T(8,128)}) custom-call(f32[512,512]{1,0:T(8,128)} %get-tuple-element.60.v_ref, f32[256,128]{1,0:T(8,128)} %bitcast.44, bf16[4,512,128]{2,1,0:T(8,128)(2,1)} %constant.33.clone.ch_ref, bf16[4,512,128]{2,1,0:T(8,128)(2,1)} %constant.34.clone.cl_ref, ...), custom_call_target="tpu_custom_call" | custom-call | flops 800000000 | bytes 4500000 | tf_op jit(solution)/shard_map/line_back/pallas_call | solution.py:638
  161.8 32.3 %sum_gradients.1 = f32[4,32,8,128]{3,2,1,0:T(8,128)} custom-call(f32[4,32,8,128]{3,2,1,0:T(8,128)} %bitcast.40), custom_call_target="tpu_custom_call" | custom-call | tf_op jit(solution)/shard_map/sum_gradients/pallas_call | solution.py:807
  194.2 1.0 slice_bitcast_fusion.1
  195.2 0.8 fusion.1
  196.0 1.6 collective-permute-start.14
  197.6 2.1 collective-permute-start.15
  201.6 9.1 %collective-permute-done.13.refs_1_ = f32[32,16,128]{2,1,0:T(8,128)S(1)} collective-permute-done((f32[32,16,128]{2,1,0:T(8,128)}, f32[32,16,128]{2,1,0:T(8,128)S(1)}, u32[]{:S(2)}, u32[]{:S(2)}) %collective-permute-start.13) | collective-permute-done | bytes 262176 | tf_op jit(solution)/shard_map/ppermute | solution.py:901
  212.2 4.7 %finish.1 = (f32[5,2048,128]{2,1,0:T(8,128)}, f32[2048,128]{1,0:T(8,128)}) custom-call(f32[32,16,128]{2,1,0:T(8,128)} %bitcast.43, f32[32,16,128]{2,1,0:T(8,128)} %copy-done.7, f32[32,16,128]{2,1,0:T(8,128)} %copy-done.8, f32[32,16,128]{2,1,0:T(8,128)} %copy-done.9, ...), custom_call_target="tpu_custom_call", output_to_operand_aliasing={{0}: (9, {})} | custom-call | flops 50000000 | bytes 4200000 | tf_op jit(solution)/shard_map/finish/pallas_call | solution.py:878
  (58 shorter events, 7.3 us)
Async XLA Ops:
  4.2 17.7 %collective-permute-start = (f32[32,16,128]{2,1,0:T(8,128)}, f32[32,16,128]{2,1,0:T(8,128)S(1)}, u32[]{:S(2)}, u32[]{:S(2)}) collective-permute-start(f32[32,16,128]{2,1,0:T(8,128)} %get-tuple-element.39), channel_id=1, source_target_pairs={{0,32},{32,64},{64,96},{96,0},{1,33},{33,65},{65,97},{97,1},{2,34}... | collective-permute-start | bytes 786440 | tf_op jit(solution)/shard_map/ppermute | solution.py:901
  6.2 17.0 %collective-permute-start.1 = (f32[32,16,128]{2,1,0:T(8,128)}, f32[32,16,128]{2,1,0:T(8,128)S(1)}, u32[]{:S(2)}, u32[]{:S(2)}) collective-permute-start(f32[32,16,128]{2,1,0:T(8,128)} %get-tuple-element.40), channel_id=1, source_target_pairs={{0,64},{32,96},{64,0},{96,32},{1,65},{33,97},{65,1},{97,33},{2,66}... | collective-permute-start | bytes 786440 | tf_op jit(solution)/shard_map/ppermute | solution.py:901
  9.8 18.0 %collective-permute-start.2 = (f32[32,16,128]{2,1,0:T(8,128)}, f32[32,16,128]{2,1,0:T(8,128)S(1)}, u32[]{:S(2)}, u32[]{:S(2)}) collective-permute-start(f32[32,16,128]{2,1,0:T(8,128)} %get-tuple-element.41), channel_id=1, source_target_pairs={{0,96},{32,0},{64,32},{96,64},{1,97},{33,1},{65,33},{97,65},{2,98}... | collective-permute-start | bytes 786440 | tf_op jit(solution)/shard_map/ppermute | solution.py:901
  10.8 52.1 %copy-start.10 = (bf16[256,63]{0,1:T(8,128)(2,1)S(1)}, bf16[256,63]{0,1:T(8,128)(2,1)}, u32[]{:S(2)}) copy-start(bf16[256,63]{0,1:T(8,128)(2,1)} %param.27) | copy-start | bytes 96772
  10.8 52.3 %copy-start.11 = (f32[256]{0:T(256)S(1)}, f32[256]{0:T(256)}, u32[]{:S(2)}) copy-start(f32[256]{0:T(256)} %param.26) | copy-start | bytes 3076
  19.2 45.3 %collective-permute-start.8 = (f32[968,128]{1,0:T(8,128)}, f32[968,128]{1,0:T(8,128)S(1)}, u32[]{:S(2)}, u32[]{:S(2)}) collective-permute-start(f32[968,128]{1,0:T(8,128)} %get-tuple-element.50), channel_id=1, source_target_pairs={{0,1},{1,2},{2,3},{3,4},{4,5},{5,6},{6,7},{7,8},{8,9},{9,10},{10,1... | collective-permute-start | bytes 1486856 | tf_op jit(solution)/shard_map/ppermute | solution.py:920
  20.6 43.9 %collective-permute-start.9 = (f32[968,128]{1,0:T(8,128)}, f32[968,128]{1,0:T(8,128)S(1)}, u32[]{:S(2)}, u32[]{:S(2)}) collective-permute-start(f32[968,128]{1,0:T(8,128)} %get-tuple-element.51), channel_id=1, source_target_pairs={{1,0},{2,1},{3,2},{4,3},{5,4},{6,5},{7,6},{8,7},{9,8},{10,9},{11,1... | collective-permute-start | bytes 1486856 | tf_op jit(solution)/shard_map/ppermute | solution.py:921
  21.9 5.9 %copy-start.14 = (f32[32,16,128]{2,1,0:T(8,128)}, f32[32,16,128]{2,1,0:T(8,128)S(1)}, u32[]{:S(2)}) copy-start(f32[32,16,128]{2,1,0:T(8,128)S(1)} %collective-permute-done) | copy-start | bytes 786436
  21.9 38.3 %collective-permute-start.6 = (f32[656,128]{1,0:T(8,128)}, f32[656,128]{1,0:T(8,128)S(1)}, u32[]{:S(2)}, u32[]{:S(2)}) collective-permute-start(f32[656,128]{1,0:T(8,128)} %get-tuple-element.49.own_ref), channel_id=1, source_target_pairs={{32,0},{64,32},{96,64},{33,1},{65,33},{97,65},{34,2},{66,34},{98,6... | collective-permute-start | bytes 1007624 | tf_op jit(solution)/shard_map/ppermute | solution.py:923
  23.2 4.6 %copy-start.15 = (f32[32,16,128]{2,1,0:T(8,128)}, f32[32,16,128]{2,1,0:T(8,128)S(1)}, u32[]{:S(2)}) copy-start(f32[32,16,128]{2,1,0:T(8,128)S(1)} %collective-permute-done.1) | copy-start | bytes 786436
  23.2 37.1 %collective-permute-start.7 = (f32[656,128]{1,0:T(8,128)}, f32[656,128]{1,0:T(8,128)S(1)}, u32[]{:S(2)}, u32[]{:S(2)}) collective-permute-start(f32[656,128]{1,0:T(8,128)} %get-tuple-element.49.own_ref), channel_id=1, source_target_pairs={{0,32},{32,64},{64,96},{1,33},{33,65},{65,97},{2,34},{34,66},{66,9... | collective-permute-start | bytes 1007624 | tf_op jit(solution)/shard_map/ppermute | solution.py:922
  27.8 0.7 copy-start.16
  59.1 56.4 %collective-permute-start.3 = (f32[32,16,128]{2,1,0:T(8,128)}, f32[32,16,128]{2,1,0:T(8,128)S(1)}, u32[]{:S(2)}, u32[]{:S(2)}) collective-permute-start(f32[32,16,128]{2,1,0:T(8,128)} %bitcast.53), channel_id=1, source_target_pairs={{0,32},{32,64},{64,96},{96,0},{1,33},{33,65},{65,97},{97,1},{2,34}... | collective-permute-start | bytes 786440 | tf_op jit(solution)/shard_map/ppermute | solution.py:901
  60.2 4.4 %copy-start.2 = (f32[656,128]{1,0:T(8,128)}, f32[656,128]{1,0:T(8,128)S(1)}, u32[]{:S(2)}) copy-start(f32[656,128]{1,0:T(8,128)S(1)} %collective-permute-done.6.east_ref) | copy-start | bytes 1007620
  60.2 65.0 %collective-permute-start.4 = (f32[32,16,128]{2,1,0:T(8,128)}, f32[32,16,128]{2,1,0:T(8,128)S(1)}, u32[]{:S(2)}, u32[]{:S(2)}) collective-permute-start(f32[32,16,128]{2,1,0:T(8,128)} %bitcast.52), channel_id=1, source_target_pairs={{0,64},{32,96},{64,0},{96,32},{1,65},{33,97},{65,1},{97,33},{2,66}... | collective-permute-start | bytes 786440 | tf_op jit(solution)/shard_map/ppermute | solution.py:901
  60.3 4.2 %copy-start.3 = (f32[656,128]{1,0:T(8,128)}, f32[656,128]{1,0:T(8,128)S(1)}, u32[]{:S(2)}) copy-start(f32[656,128]{1,0:T(8,128)S(1)} %collective-permute-done.7.west_ref) | copy-start | bytes 1007620
  60.3 64.8 %collective-permute-start.5 = (f32[32,16,128]{2,1,0:T(8,128)}, f32[32,16,128]{2,1,0:T(8,128)S(1)}, u32[]{:S(2)}, u32[]{:S(2)}) collective-permute-start(f32[32,16,128]{2,1,0:T(8,128)} %bitcast.51), channel_id=1, source_target_pairs={{0,96},{32,0},{64,32},{96,64},{1,97},{33,1},{65,33},{97,65},{2,98}... | collective-permute-start | bytes 786440 | tf_op jit(solution)/shard_map/ppermute | solution.py:901
  64.5 0.8 copy-start
  64.5 1.0 copy-start.1
  112.7 23.3 %collective-permute-start.10 = (f32[32,16,128]{2,1,0:T(8,128)}, f32[32,16,128]{2,1,0:T(8,128)S(1)}, u32[]{:S(2)}, u32[]{:S(2)}) collective-permute-start(f32[32,16,128]{2,1,0:T(8,128)} %get-tuple-element.57), channel_id=1, source_target_pairs={{0,32},{32,64},{64,96},{96,0},{1,33},{33,65},{65,97},{97,1},{2,34}... | collective-permute-start | bytes 786440 | tf_op jit(solution)/shard_map/ppermute | solution.py:901
  113.1 22.9 %collective-permute-start.11 = (f32[32,16,128]{2,1,0:T(8,128)}, f32[32,16,128]{2,1,0:T(8,128)S(1)}, u32[]{:S(2)}, u32[]{:S(2)}) collective-permute-start(f32[32,16,128]{2,1,0:T(8,128)} %get-tuple-element.58), channel_id=1, source_target_pairs={{0,64},{32,96},{64,0},{96,32},{1,65},{33,97},{65,1},{97,33},{2,66}... | collective-permute-start | bytes 786440 | tf_op jit(solution)/shard_map/ppermute | solution.py:901
  115.5 9.6 %copy-start.4 = (f32[32,16,128]{2,1,0:T(8,128)}, f32[32,16,128]{2,1,0:T(8,128)S(1)}, u32[]{:S(2)}) copy-start(f32[32,16,128]{2,1,0:T(8,128)S(1)} %collective-permute-done.3.refs_1_) | copy-start | bytes 786436
  115.5 20.4 %collective-permute-start.12 = (f32[32,16,128]{2,1,0:T(8,128)}, f32[32,16,128]{2,1,0:T(8,128)S(1)}, u32[]{:S(2)}, u32[]{:S(2)}) collective-permute-start(f32[32,16,128]{2,1,0:T(8,128)} %get-tuple-element.59), channel_id=1, source_target_pairs={{0,96},{32,0},{64,32},{96,64},{1,97},{33,1},{65,33},{97,65},{2,98}... | collective-permute-start | bytes 786440 | tf_op jit(solution)/shard_map/ppermute | solution.py:901
  125.1 0.8 copy-start.6
  135.9 0.7 copy-start.12
  135.9 0.8 copy-start.13
  136.0 0.9 copy-start.17
  196.0 14.7 %collective-permute-start.13 = (f32[32,16,128]{2,1,0:T(8,128)}, f32[32,16,128]{2,1,0:T(8,128)S(1)}, u32[]{:S(2)}, u32[]{:S(2)}) collective-permute-start(f32[32,16,128]{2,1,0:T(8,128)} %bitcast.64), channel_id=1, source_target_pairs={{0,32},{32,64},{64,96},{96,0},{1,33},{33,65},{65,97},{97,1},{2,34}... | collective-permute-start | bytes 786440 | tf_op jit(solution)/shard_map/ppermute | solution.py:901
  196.0 14.7 %collective-permute-start.14 = (f32[32,16,128]{2,1,0:T(8,128)}, f32[32,16,128]{2,1,0:T(8,128)S(1)}, u32[]{:S(2)}, u32[]{:S(2)}) collective-permute-start(f32[32,16,128]{2,1,0:T(8,128)} %bitcast.61), channel_id=1, source_target_pairs={{0,64},{32,96},{64,0},{96,32},{1,65},{33,97},{65,1},{97,33},{2,66}... | collective-permute-start | bytes 786440 | tf_op jit(solution)/shard_map/ppermute | solution.py:901
  197.6 13.7 %collective-permute-start.15 = (f32[32,16,128]{2,1,0:T(8,128)}, f32[32,16,128]{2,1,0:T(8,128)S(1)}, u32[]{:S(2)}, u32[]{:S(2)}) collective-permute-start(f32[32,16,128]{2,1,0:T(8,128)} %bitcast.59), channel_id=1, source_target_pairs={{0,96},{32,0},{64,32},{96,64},{1,97},{33,1},{65,33},{97,65},{2,98}... | collective-permute-start | bytes 786440 | tf_op jit(solution)/shard_map/ppermute | solution.py:901
  210.7 0.7 copy-start.7
  210.7 0.8 copy-start.8
  (2 other events, 1.4 us)
